TPU v7x, 1024 devices: a whole 4x8x16 slice. The times are simulated.
1024 devices in a mesh: lat: 16 (over z), wave: 64 (over x, y, core).
Axes of the slice: x: 4, y: 8, z: 16, core: 2. Of those that a mesh axis runs over, the one named last changes fastest.
Arguments:
- fourier_in: bfloat16 [64, 1280, 1280], P('wave', 'lat'), may hold values from -6 to 6
- legendre: bfloat16 [640, 1280, 1281], P('wave', 'lat'), may hold values from -0.15625 to 0.15625
- quad_weights: float32 [1280], P('lat'), may hold values from 0.3 to 3
- si_coeffs: float32 [2, 8], replicated, may hold values from 0.25 to 4
- owner_table: int32 [640], replicated, may hold values from 0 to 639, each once
Outputs:
- spectral: float32 [16, 2, 640, 1281], P('lat', None, 'wave')
- fourier_out: bfloat16 [64, 1280, 1280], P('wave', 'lat')
Inputs may be any that keep to these rules, and one draw needn't show every extreme that they name: owner_table is a permutation: slot s holds zonal wavenumbers owner_table[s] and 1279 - owner_table[s], so every wavenumber is held by exactly one slot.
All inputs are finite; a program needn't handle non-finite values.
Results may differ from a plain program's by a relative error of at most 0.017.
Values may be sent and summed in bfloat16 or wider, within the bound.
No kernel may reach another device: no remote copies, remote signals or barrier semaphores. Data moves between devices by JAX's collectives and lax.ppermute only.
A program may use at most 32 MiB of HBM per device.

v0:
```python
import jax
import jax.numpy as jnp
from jax import lax
from jax.sharding import PartitionSpec as P

TRUNC = 1279
MODES = 8
M = 1280
PAIRS = 640
NP = 1281
CHANNELS = 16


def pair_layout(lowest):
    column = jnp.arange(NP, dtype=jnp.int32)
    first_part = column[None, :] < M - lowest[:, None]
    degree = jnp.where(first_part, lowest[:, None] + column[None, :], column[None, :] - 1)
    wave_order = jnp.where(first_part, lowest[:, None], TRUNC - lowest[:, None])
    parity_sign = 1.0 - 2.0 * ((degree + wave_order) % 2).astype(jnp.float32)
    part_mask = jnp.stack([first_part, jnp.logical_not(first_part)], axis=0).astype(jnp.float32)
    hemi_sign = jnp.stack([jnp.ones_like(parity_sign), parity_sign], axis=0)
    return (degree, hemi_sign[:, None, :, :] * part_mask[None, :, :, :])


def implicit_solve(raw, coupling, depth, degree):
    degree_f = degree.astype(jnp.float32)
    degree_scale = (degree_f * (degree_f + 1.0) / float(TRUNC * (TRUNC + 1)))[None, :, :]
    coupling_b = coupling[:, None, None]
    depth_b = depth[:, None, None]
    divergence = (raw[:, 0] + coupling_b * degree_scale * raw[:, 1]) / (
        1.0 + coupling_b * depth_b * degree_scale
    )
    geopotential = raw[:, 1] - depth_b * divergence
    return jnp.stack([divergence, geopotential], axis=1)


def body(fourier_in, legendre, quad_weights, si_coeffs, owner_table):
    lat_index = lax.axis_index("lat")
    wave_index = lax.axis_index("wave")
    slot_count = legendre.shape[0]
    band_loops = legendre.shape[1]
    loop_index = lat_index * band_loops + jnp.arange(band_loops, dtype=jnp.int32)
    wavenumber = jnp.arange(M, dtype=jnp.int32)
    carried = wavenumber[None, :] <= 2 * loop_index[:, None] + 9
    weighted = jnp.where(
        carried[None, :, :], fourier_in.astype(jnp.float32) * quad_weights[None, :, None], 0.0
    ).astype(jnp.bfloat16)
    pair_order = jnp.stack([owner_table, TRUNC - owner_table], axis=1).reshape(2 * PAIRS)
    ordered = jnp.take(weighted, pair_order, axis=2)
    received = lax.all_to_all(ordered, "wave", split_axis=2, concat_axis=0, tiled=True)
    received = received.reshape(2, CHANNELS, 2, band_loops, slot_count, 2)
    lowest = lax.dynamic_slice_in_dim(owner_table, wave_index * slot_count, slot_count, 0)
    degree, factors = pair_layout(lowest)
    projected = jnp.einsum(
        "hcrjst,sjn->htcrsn", received, legendre, preferred_element_type=jnp.float32
    )
    partial_sums = jnp.sum(projected * factors[:, :, None, None, :, :], axis=(0, 1))
    partial_sums = partial_sums.reshape(MODES, 2, 2, slot_count, NP)
    partial_sums = jnp.transpose(partial_sums, (0, 2, 1, 3, 4)).reshape(
        2 * MODES, 2, slot_count, NP
    )
    shares = lax.psum_scatter(
        partial_sums.astype(jnp.bfloat16), "lat", scatter_dimension=0, tiled=True
    ).astype(jnp.float32)
    local_count = shares.shape[0]
    mode_of_item = (lat_index * local_count + jnp.arange(local_count, dtype=jnp.int32)) // 2
    spectral = implicit_solve(
        shares, jnp.take(si_coeffs[0], mode_of_item), jnp.take(si_coeffs[1], mode_of_item), degree
    )
    spectral_half = lax.all_gather(spectral.astype(jnp.bfloat16), "lat", axis=0, tiled=True)
    spec_fields = spectral_half.reshape(MODES, 2, 2, slot_count, NP)
    spec_fields = jnp.transpose(spec_fields, (0, 2, 1, 3, 4)).reshape(CHANNELS, 2, slot_count, NP)
    signed = factors.astype(jnp.bfloat16)[:, :, None, None, :, :] * spec_fields[None, None]
    synthesis = jnp.einsum(
        "htcrsn,sjn->hcrjst", signed, legendre, preferred_element_type=jnp.float32
    )
    synthesis = synthesis.astype(jnp.bfloat16).reshape(4 * CHANNELS, band_loops, 2 * slot_count)
    arrived = lax.all_to_all(synthesis, "wave", split_axis=0, concat_axis=2, tiled=True)
    slot_of_pair = jnp.argsort(owner_table)
    lower_half = wavenumber < PAIRS
    pair_index = jnp.where(lower_half, wavenumber, TRUNC - wavenumber)
    column_index = 2 * jnp.take(slot_of_pair, pair_index) + jnp.where(lower_half, 0, 1)
    fourier_out = jnp.take(arrived, column_index, axis=2)
    fourier_out = jnp.where(carried[None, :, :], fourier_out, jnp.zeros_like(fourier_out))
    return (spectral, fourier_out)


def solution(mesh):
    in_specs = (P("wave", "lat", None), P("wave", "lat", None), P("lat"), P(), P())
    out_specs = (P("lat", None, "wave", None), P("wave", "lat", None))
    return jax.shard_map(body, mesh=mesh, in_specs=in_specs, out_specs=out_specs, check_vma=False)
```

profile of v0, /device:TPU:1, one launch (start us, length us, event | category | flops | bytes accessed | tf_op | source)
XLA Modules:
  0.0 285.8 jit_solution(465603934295947242)
XLA Ops:
  7.2 0.0 copy-start
  7.2 0.8 broadcast_subtract_fusion
  8.0 0.7 stack.23
  8.7 0.2 copy.28
  8.9 0.2 reshape.607
  9.1 1.1 copy.29
  10.3 0.8 fusion.18
  11.1 2.8 gather_fusion.1
  13.9 0.0 copy-start.2
  14.0 0.2 bitcast_select_fusion.1
  14.2 5.1 %copy.45 = bf16[1,80,1280]{1,0,2:T(2,128)(2,1)S(1)} copy(bf16[1,80,1280]{1,2,0:T(8,128)(2,1)S(1)} %bitcast_select_fusion.1) | data formatting | bytes 409600 | tf_op jit(solution)/shard_map/jit(_take)/select_n | solution.py:49
  19.3 0.5 broadcast.558
  19.8 7.5 %reduce.4 = bf16[1280,80]{1,0:T(8,128)(2,1)S(1)} reduce(bf16[1280,1,80]{2,1,0:T(2,128)(2,1)S(1)} %bitcast.63, bf16[]{:T(256)} %broadcast.558), dimensions={1}, to_apply=%bitcast.58.reduce_sub_computation | reduce | bytes 409602
  27.3 1.2 reshape.714
  28.5 18.2 %all-to-all-start = ((bf16[64,2,800]{2,1,0:T(2,128)(2,1)}), bf16[64,2,800]{2,1,0:T(2,128)(2,1)S(1)}, u32[]{:S(2)}, u32[]{:S(2)}) async-start(bf16[64,2,800]{2,1,0:T(2,128)(2,1)} %reshape.714), calls=%async_computation | async-start | bytes 458752 | tf_op jit(solution)/shard_map/all_to_all | solution.py:50
  46.7 0.2 all-reduce.4.cloned.1.call-start
  46.9 0.0 copy-done.2
  46.9 0.1 broadcast_subtract_fusion.1
  47.0 0.2 iota_compare_fusion.1
  47.2 0.1 add_convert_fusion
  47.3 0.4 fusion.22
  47.7 0.1 stack.26
  47.8 0.8 fusion.32
  48.6 9.3 %all-to-all-done = bf16[64,2,800]{2,1,0:T(2,128)(2,1)S(1)} async-done(((bf16[64,2,800]{2,1,0:T(2,128)(2,1)}), bf16[64,2,800]{2,1,0:T(2,128)(2,1)S(1)}, u32[]{:S(2)}, u32[]{:S(2)}) %all-to-all-start) | async-done | bytes 204832 | tf_op jit(solution)/shard_map/all_to_all | solution.py:50
  57.9 0.6 reshape.715
  58.5 4.8 %bitcast_reduce_fusion = bf16[80,1280]{0,1:T(8,128)(2,1)S(1)} fusion(bf16[1280,1,80]{2,1,0:T(2,128)(2,1)S(1)} %reshape.715), kind=kLoop, calls=%fused_computation.71 | loop fusion | bytes 409600 | tf_op jit(solution)/shard_map/all_to_all | solution.py:50
  63.3 0.1 all_to_all.25
  63.4 0.1 copy.31
  63.5 0.0 copy-done
  63.5 1.1 fusion
  64.6 0.0 copy-start.3
  64.6 0.7 copy.33
  65.3 1.7 copy.34
  67.0 0.0 all-reduce.4.cloned.1.call-update
  67.0 0.0 copy-done.3
  67.0 0.7 fusion.37
  67.7 0.6 fusion.38
  70.2 4.4 %sort.17 = (s32[640]{0:T(1024)}, s32[640]{0:T(1024)S(1)}) sort(s32[640]{0:T(1024)S(1)} %copy-done.2, s32[640]{0:T(1024)S(1)} %iota.74), dimensions={0}, to_apply=%region_2.4 | sort | flops 6400 | bytes 10240 | tf_op jit(solution)/shard_map/jit(argsort)/sort | solution.py:79
  74.5 1.3 dynamic-slice.8
  75.8 124.2 %all-reduce.4.cloned.1.call-done = bf16[16,2,10,1281]{3,1,2,0:T(2,128)(2,1)} async-done(((bf16[16,2,10,1281]{3,1,2,0:T(2,128)(2,1)}), bf16[16,2,10,1281]{3,1,2,0:T(2,128)(2,1)}) %all-reduce.4.cloned.1.call-update) | async-done | bytes 819856
  200.0 1.5 dynamic-slice_convert_fusion
  201.5 1.1 multiply_subtract_fusion
  202.6 0.8 fusion.34
  203.4 0.0 copy-start.1
  203.4 27.2 %all_gather.3 = bf16[16,2,10,1281]{3,1,2,0:T(2,128)(2,1)S(1)} all-gather(bf16[1,2,10,1281]{3,1,2,0:T(2,128)(2,1)S(1)} %get-tuple-element.37), channel_id=1, replica_groups=mesh['lat'=16,'wave'=64] {'lat'}, dimensions={0}, use_global_device_ids=true | all-gather | bytes 871080 | tf_op jit(solution)/shard_map/all_gather | solution.py:70
  230.5 0.7 copy.35
  231.2 0.1 copy.36
  231.3 0.0 copy-done.1
  231.3 1.1 fusion.12
  232.5 0.3 copy.37
  232.8 1.0 copy.38
  233.8 26.6 %all-to-all-start.1 = ((bf16[64,80,20]{1,2,0:T(8,128)(2,1)}), bf16[64,80,20]{1,2,0:T(8,128)(2,1)S(1)}, u32[]{:S(2)}, u32[]{:S(2)}) async-start(bf16[64,80,20]{1,2,0:T(8,128)(2,1)} %copy.38), calls=%async_computation.1 | async-start | bytes 786432 | tf_op jit(solution)/shard_map/all_to_all | solution.py:78
  260.4 5.0 %gather_fusion = s32[1280]{0:T(1024)S(1)} fusion(s32[640]{0:T(1024)S(1)} %get-tuple-element.4, s32[2048]{0:T(1024)S(1)} %pad_clamp_fusion.1), kind=kCustom, calls=%fused_computation.2 | custom fusion | bytes 15360 | tf_op jit(solution)/shard_map/jit(_take)/gather | solution.py:82
  265.4 9.5 %all-to-all-done.1 = bf16[64,80,20]{1,2,0:T(8,128)(2,1)S(1)} async-done(((bf16[64,80,20]{1,2,0:T(8,128)(2,1)}), bf16[64,80,20]{1,2,0:T(8,128)(2,1)S(1)}, u32[]{:S(2)}, u32[]{:S(2)}) %all-to-all-start.1) | async-done | bytes 204832 | tf_op jit(solution)/shard_map/all_to_all | solution.py:78
  274.9 0.1 reshape.705
  275.0 2.8 gather_fusion.2
  277.9 0.2 fusion.17
  278.1 0.9 copy.39
  (14 shorter events, 0.1 us)
Async XLA Ops:
  7.2 56.3 %copy-start = (bf16[10,80,1281]{2,1,0:T(8,128)(2,1)S(1)}, bf16[10,80,1281]{2,1,0:T(8,128)(2,1)}, u32[]{:S(2)}) copy-start(bf16[10,80,1281]{2,1,0:T(8,128)(2,1)} %param.8) | copy-start | bytes 6148804
  13.9 33.0 %copy-start.2 = (s32[640]{0:T(1024)S(1)}, s32[640]{0:T(1024)}, u32[]{:S(2)}) copy-start(s32[640]{0:T(1024)} %param.11) | copy-start | bytes 7684
  28.5 29.4 %all-to-all-start = ((bf16[64,2,800]{2,1,0:T(2,128)(2,1)}), bf16[64,2,800]{2,1,0:T(2,128)(2,1)S(1)}, u32[]{:S(2)}, u32[]{:S(2)}) async-start(bf16[64,2,800]{2,1,0:T(2,128)(2,1)} %reshape.714), calls=%async_computation | async-start | bytes 458752 | tf_op jit(solution)/shard_map/all_to_all | solution.py:50
  46.7 153.3 %all-reduce.4.cloned.1.call-start = ((), (), s32[]{:S(2)}) async-start(), calls=%async_computation.2 | async-start | bytes 1802240
  64.6 2.4 copy-start.3
  203.4 28.0 %copy-start.1 = (bf16[2,2,10,1281]{3,1,0,2:T(2,128)(2,1)S(1)}, bf16[2,2,10,1281]{3,1,0,2:T(2,128)(2,1)}, u32[]{:S(2)}) copy-start(bf16[2,2,10,1281]{3,1,0,2:T(2,128)(2,1)} %get-tuple-element.43) | copy-start | bytes 307444
  233.8 41.1 %all-to-all-start.1 = ((bf16[64,80,20]{1,2,0:T(8,128)(2,1)}), bf16[64,80,20]{1,2,0:T(8,128)(2,1)S(1)}, u32[]{:S(2)}, u32[]{:S(2)}) async-start(bf16[64,80,20]{1,2,0:T(8,128)(2,1)} %copy.38), calls=%async_computation.1 | async-start | bytes 786432 | tf_op jit(solution)/shard_map/all_to_all | solution.py:78
Sparse Core Ops, SparseCore 0:
  67.1 132.8 all-reduce.3
where the time goes:
time: 286 us
  waiting for transfers between devices  143 us (50%)
  starting transfers between devices  45 us (16%)
  local copies, waits for them, and re-layouts  32 us (11%)
  blocking collectives  27.2 us (10%)
  other arithmetic  20.2 us (7%)
  between operations  16.2 us (6%)
    unnamed x2, waiting for transfers between devices  124 us
    all_gather x1, blocking collectives, body(): lax.all_gather(spectral.astype(jnp.bfloat16), 'lat', axis=0, tiled=True)  27.2 us
    all_to_all x1, starting transfers between devices, body(): lax.all_to_all(synthesis, 'wave', split_axis=0, concat_axis=2, tiled=True)  26.6 us
    all_to_all x1, starting transfers between devices, body(): lax.all_to_all(ordered, 'wave', split_axis=2, concat_axis=0, tiled=True)  18.2 us
    all_to_all x1, waiting for transfers between devices, body(): lax.all_to_all(synthesis, 'wave', split_axis=0, concat_axis=2, tiled=True)  9.52 us
    all_to_all x1, waiting for transfers between devices, body(): lax.all_to_all(ordered, 'wave', split_axis=2, concat_axis=0, tiled=True)  9.32 us
    unnamed x1, other arithmetic  7.45 us
  transfers between devices with their start and end apart: 3, of which 3 were waited for; matrix products, arithmetic and copies ran while one was open for 5% of the time, Pallas kernels for 0%

commit v1 on v0

v1 whole, which is shorter than its diff:
```python
import jax
import jax.numpy as jnp
from jax import lax
from jax.sharding import PartitionSpec as P

TRUNC = 1279
MODES = 8
M = 1280
PAIRS = 640
NP = 1281
CHANNELS = 16
WAVE = 64
SLOTS = 10
HALF = 12


def pair_layout(lowest):
    column = jnp.arange(NP, dtype=jnp.int32)
    first_part = column[None, :] < M - lowest[:, None]
    degree = jnp.where(first_part, lowest[:, None] + column[None, :], column[None, :] - 1)
    wave_order = jnp.where(first_part, lowest[:, None], TRUNC - lowest[:, None])
    parity_sign = 1.0 - 2.0 * ((degree + wave_order) % 2).astype(jnp.float32)
    part_mask = jnp.stack([first_part, jnp.logical_not(first_part)], axis=0).astype(jnp.float32)
    hemi_sign = jnp.stack([jnp.ones_like(parity_sign), parity_sign], axis=0)
    return (degree, hemi_sign[:, None, :, :] * part_mask[None, :, :, :])


def implicit_solve(raw, coupling, depth, degree):
    degree_f = degree.astype(jnp.float32)
    scale = degree_f * (degree_f + 1.0) / float(TRUNC * (TRUNC + 1))
    divergence = (raw[0] + coupling * scale * raw[1]) / (1.0 + coupling * depth * scale)
    geopotential = raw[1] - depth * divergence
    return divergence, geopotential


def body(fourier_in, legendre, quad_weights, si_coeffs, owner_table):
    lat_index = lax.axis_index("lat")
    wave_index = lax.axis_index("wave")
    band_loops = legendre.shape[1]
    loop_index = lat_index * band_loops + jnp.arange(band_loops, dtype=jnp.int32)
    wavenumber = jnp.arange(M, dtype=jnp.int32)
    carried = wavenumber[None, :] <= 2 * loop_index[:, None] + 9
    weighted = jnp.where(
        carried, fourier_in[0].astype(jnp.float32) * quad_weights[:, None], 0.0
    ).astype(jnp.bfloat16)
    low = jnp.pad(owner_table.reshape(WAVE, SLOTS), ((0, 0), (0, HALF - SLOTS)), constant_values=-1)
    order = jnp.concatenate([low, jnp.where(low < 0, -1, TRUNC - low)], axis=1).reshape(-1)
    select = (order[:, None] == wavenumber[None, :]).astype(jnp.bfloat16)
    ordered = lax.dot_general(
        select, weighted, (((1,), (1,)), ((), ())), preferred_element_type=jnp.float32
    ).astype(jnp.bfloat16).reshape(WAVE, 2 * HALF, band_loops)
    received = lax.all_to_all(ordered, "wave", split_axis=0, concat_axis=0, tiled=True)
    received = received.reshape(2, MODES, 2, 2, 2, HALF, band_loops)[:, :, :, :, :, :SLOTS]
    lowest = lax.dynamic_slice_in_dim(owner_table, wave_index * SLOTS, SLOTS, 0)
    degree, factors = pair_layout(lowest)
    partial_sums = jnp.einsum(
        "hkfrtsj,sjn,htsn->krsfn", received, legendre, factors.astype(jnp.bfloat16),
        preferred_element_type=jnp.float32,
    ).astype(jnp.bfloat16).reshape(2 * MODES, SLOTS, 2, NP)
    bands = lax.all_to_all(partial_sums, "lat", split_axis=0, concat_axis=0, tiled=True)
    raw = jnp.sum(bands.astype(jnp.float32), axis=0)
    mode = lat_index // 2
    divergence, geopotential = implicit_solve(
        (raw[:, 0], raw[:, 1]), si_coeffs[0, mode], si_coeffs[1, mode], degree
    )
    spectral = jnp.stack([divergence, geopotential], axis=0)[None]
    half = jnp.stack([divergence, geopotential], axis=1).astype(jnp.bfloat16)[None]
    gathered = lax.all_gather(half, "lat", axis=0, tiled=True)
    fields = gathered.reshape(MODES, 2, SLOTS, 2, NP)
    signed = factors.astype(jnp.bfloat16)[:, :, None, None, None] * jnp.transpose(fields, (0, 3, 1, 2, 4))[None, None]
    synthesis = jnp.einsum(
        "htkfrsn,sjn->hkfrtsj", signed, legendre, preferred_element_type=jnp.float32
    ).astype(jnp.bfloat16)
    synthesis = jnp.pad(synthesis, ((0, 0),) * 5 + ((0, HALF - SLOTS), (0, 0)))
    synthesis = synthesis.reshape(WAVE, 2 * HALF, band_loops)
    arrived = lax.all_to_all(synthesis, "wave", split_axis=0, concat_axis=0, tiled=True)
    fourier_out = lax.dot_general(
        arrived.reshape(WAVE * 2 * HALF, band_loops), select, (((0,), (0,)), ((), ())),
        preferred_element_type=jnp.float32,
    ).astype(jnp.bfloat16)
    fourier_out = jnp.where(carried, fourier_out, jnp.zeros_like(fourier_out))[None]
    return (spectral, fourier_out)


def solution(mesh):
    in_specs = (P("wave", "lat", None), P("wave", "lat", None), P("lat"), P(), P())
    out_specs = (P("lat", None, "wave", None), P("wave", "lat", None))
    return jax.shard_map(body, mesh=mesh, in_specs=in_specs, out_specs=out_specs, check_vma=False)
```

time: 286 us -> 163 us (0.57)
  waiting for transfers between devices: 143 us -> 62.5 us
  local copies, waits for them, and re-layouts: 32 us -> 6.52 us
  other arithmetic: 20.2 us -> 5.45 us
  between operations: 16.2 us -> 2.83 us
  matrix products: 2.23 us -> 7.33 us
  blocking collectives: 27.2 us -> 31.2 us
    unnamed x2 -> x0, waiting for transfers between devices: 124 us -> none
    all_to_all x2 -> x3, waiting for transfers between devices: 18.8 us -> 62.5 us  [the longest x1 36.8 us: body(): lax.all_to_all(partial_sums, 'lat', split_axis=0, concat_axis=0, tiled=True)]
    gather x3 -> x0, local copies, waits for them, and re-layouts: 10.6 us -> none  [the longest x1 4.97 us: body(): jnp.take(slot_of_pair, pair_index)]
    unnamed x1, other arithmetic: 7.45 us -> 0.14 us
    select_n x1 -> x0, local copies, waits for them, and re-layouts: 5.11 us -> none  [body(): ordered = jnp.take(weighted, pair_order, axis=2)]
    dot_general x2 -> x4, matrix products: 2.23 us -> 7.33 us  [the longest x1 2.78 us: body(): lax.dot_general(select, weighted, (((1,), (1,)), ((), ())), preferred_ele...]
    all_to_all x3 -> x1, local copies, waits for them, and re-layouts: 4.98 us -> 0.08 us  [body(): lax.all_to_all(ordered, 'wave', split_axis=0, concat_axis=0, tiled=True)]
    sort x1 -> x0, other arithmetic: 4.37 us -> none  [body(): slot_of_pair = jnp.argsort(owner_table)]
  transfers between devices with their start and end apart: 3 -> 3, of which waited for: 3 -> 3; matrix products, arithmetic and copies ran while one was open for 5% -> 2% of each run, Pallas kernels for 0% -> 0%
where the time goes in v1:
time: 163 us; the launch traced here: 162 us
  waiting for transfers between devices  62.5 us (38%)
  starting transfers between devices  46.6 us (29%)
  blocking collectives  31.2 us (19%)
  matrix products  7.33 us (4%)
  local copies, waits for them, and re-layouts  6.52 us (4%)
  other arithmetic  5.45 us (3%)
  between operations  2.83 us (2%)
    all_to_all x1, waiting for transfers between devices, body(): lax.all_to_all(partial_sums, 'lat', split_axis=0, concat_axis=0, tiled=True)  36.8 us
    all_gather x1, blocking collectives, body(): gathered = lax.all_gather(half, 'lat', axis=0, tiled=True)  31.2 us
    all_to_all x1, starting transfers between devices, body(): lax.all_to_all(ordered, 'wave', split_axis=0, concat_axis=0, tiled=True)  18.2 us
    all_to_all x1, starting transfers between devices, body(): lax.all_to_all(synthesis, 'wave', split_axis=0, concat_axis=0, tiled=True)  16.5 us
    all_to_all x1, waiting for transfers between devices, body(): lax.all_to_all(ordered, 'wave', split_axis=0, concat_axis=0, tiled=True)  13 us
    all_to_all x1, waiting for transfers between devices, body(): lax.all_to_all(synthesis, 'wave', split_axis=0, concat_axis=0, tiled=True)  12.7 us
    all_to_all x1, starting transfers between devices, body(): lax.all_to_all(partial_sums, 'lat', split_axis=0, concat_axis=0, tiled=True)  11.9 us
  transfers between devices with their start and end apart: 3, of which 3 were waited for; matrix products, arithmetic and copies ran while one was open for 2% of the time, Pallas kernels for 0%

profile of v1, /device:TPU:1, one launch (start us, length us, event | category | flops | bytes accessed | tf_op | source)
XLA Modules:
  0.0 162.4 jit_solution(8005237957237593142)
XLA Ops:
  0.6 0.0 copy-start
  0.7 1.0 reshape.629
  1.6 0.1 pad_add_fusion
  1.7 0.1 eq.17
  1.8 2.8 %fusion.7 = bf16[1536,80]{0,1:T(8,128)(2,1)S(1)} fusion(s32[1536]{0:T(1024)S(1)} %eq.17, bf16[1,80,1280]{2,1,0:T(8,128)(2,1)} %param.5, f32[80]{0:T(128)} %param.7, s32[80]{0:T(128)S(1)} %multiply_add_fusion), kind=kOutput, calls=%fused_computation.9 | convolution fusion | flops 317173760 | bytes 457344 | tf_op jit(solution)/shard_map/dot_general | solution.py:49
  4.6 0.9 copy.67
  5.5 18.2 %all-to-all-start = ((bf16[64,24,80]{2,1,0:T(8,128)(2,1)}), bf16[64,24,80]{2,1,0:T(8,128)(2,1)S(1)}, u32[]{:S(2)}, u32[]{:S(2)}) async-start(bf16[64,24,80]{2,1,0:T(8,128)(2,1)} %bitcast.3), calls=%async_computation | async-start | bytes 786432 | tf_op jit(solution)/shard_map/all_to_all | solution.py:52
  23.7 0.8 broadcast_subtract_fusion
  24.5 0.2 iota_compare_fusion.12
  24.7 0.4 fusion.35
  25.1 0.1 add_convert_fusion
  25.2 0.1 stack.23
  25.3 0.1 bitcast_convert_fusion
  25.4 13.0 %all-to-all-done = bf16[64,24,80]{2,1,0:T(8,128)(2,1)S(1)} async-done(((bf16[64,24,80]{2,1,0:T(8,128)(2,1)}), bf16[64,24,80]{2,1,0:T(8,128)(2,1)S(1)}, u32[]{:S(2)}, u32[]{:S(2)}) %all-to-all-start) | async-done | bytes 245792 | tf_op jit(solution)/shard_map/all_to_all | solution.py:52
  38.4 0.1 copy.68
  38.5 0.3 slice.12
  38.7 0.0 copy-done
  38.8 1.1 fusion.2
  39.9 0.0 copy-start.1
  39.9 1.6 %copy.88 = bf16[10,1281,8,2,2]{1,3,0,4,2:T(2,128)(2,1)} copy(bf16[10,1281,8,2,2]{1,2,4,3,0:T(8,128)(2,1)S(1)} %fusion.2) | data formatting | bytes 1639680
  41.5 11.9 %all-to-all-start.1 = ((bf16[16,10,2,1281]{3,2,1,0:T(2,128)(2,1)}), bf16[16,10,2,1281]{3,2,1,0:T(2,128)(2,1)S(1)}, u32[]{:S(2)}, u32[]{:S(2)}) async-start(bf16[16,10,2,1281]{3,2,1,0:T(2,128)(2,1)} %bitcast.59), calls=%async_computation.1 | async-start | bytes 1802240 | tf_op jit(solution)/shard_map/all_to_all | solution.py:60
  53.4 0.0 copy-done.1
  53.4 0.6 constant_dynamic-slice_fusion.1
  56.0 36.8 %all-to-all-done.1 = bf16[16,10,2,1281]{3,2,1,0:T(2,128)(2,1)S(1)} async-done(((bf16[16,10,2,1281]{3,2,1,0:T(2,128)(2,1)}), bf16[16,10,2,1281]{3,2,1,0:T(2,128)(2,1)S(1)}, u32[]{:S(2)}, u32[]{:S(2)}) %all-to-all-start.1) | async-done | bytes 819872 | tf_op jit(solution)/shard_map/all_to_all | solution.py:60
  92.8 0.8 convert_reduce_fusion
  93.5 0.4 fusion.42
  94.0 0.7 subtract_convert_fusion
  94.8 31.2 %all_gather.3 = bf16[16,10,2,1281]{3,2,1,0:T(2,128)(2,1)S(1)} all-gather(bf16[1,10,2,1281]{3,2,1,0:T(2,128)(2,1)S(1)} %copy.70), channel_id=1, replica_groups=mesh['lat'=16,'wave'=64] {'lat'}, dimensions={0}, use_global_device_ids=true | all-gather | bytes 871080 | tf_op jit(solution)/shard_map/all_gather | solution.py:68
  126.0 0.1 copy.71
  126.1 1.1 fusion.20
  127.3 0.3 copy.87
  127.6 0.4 pad.10.clone
  128.0 1.0 copy.73
  129.0 16.5 %all-to-all-start.2 = ((bf16[64,24,80]{2,1,0:T(8,128)(2,1)}), bf16[64,24,80]{2,1,0:T(8,128)(2,1)S(1)}, u32[]{:S(2)}, u32[]{:S(2)}) async-start(bf16[64,24,80]{2,1,0:T(8,128)(2,1)} %copy.73), calls=%async_computation.2 | async-start | bytes 786432 | tf_op jit(solution)/shard_map/all_to_all | solution.py:76
  145.5 1.1 bitcast_subtract_fusion
  146.6 0.8 maximum_bitcast_fusion
  147.4 12.7 %all-to-all-done.2 = bf16[64,24,80]{2,1,0:T(8,128)(2,1)S(1)} async-done(((bf16[64,24,80]{2,1,0:T(8,128)(2,1)}), bf16[64,24,80]{2,1,0:T(8,128)(2,1)S(1)}, u32[]{:S(2)}, u32[]{:S(2)}) %all-to-all-start.2) | async-done | bytes 245792 | tf_op jit(solution)/shard_map/all_to_all | solution.py:76
  160.1 2.3 %fusion.10 = bf16[1,80,1280]{2,1,0:T(8,128)(2,1)} fusion(bf16[1536,80]{1,0:T(8,128)(2,1)S(1)} %bitcast.63, s32[1536]{0:T(1024)S(1)} %eq.17, s32[80]{0:T(128)S(1)} %multiply_add_fusion), kind=kOutput, calls=%fused_computation.12 | convolution fusion | flops 316846080 | bytes 457024 | tf_op jit(solution)/shard_map/dot_general | solution.py:77
  (7 shorter events, 0.1 us)
Async XLA Ops:
  0.6 38.1 %copy-start = (bf16[10,80,1281]{2,1,0:T(8,128)(2,1)S(1)}, bf16[10,80,1281]{2,1,0:T(8,128)(2,1)}, u32[]{:S(2)}) copy-start(bf16[10,80,1281]{2,1,0:T(8,128)(2,1)} %param.6) | copy-start | bytes 6148804
  5.5 32.8 %all-to-all-start = ((bf16[64,24,80]{2,1,0:T(8,128)(2,1)}), bf16[64,24,80]{2,1,0:T(8,128)(2,1)S(1)}, u32[]{:S(2)}, u32[]{:S(2)}) async-start(bf16[64,24,80]{2,1,0:T(8,128)(2,1)} %bitcast.3), calls=%async_computation | async-start | bytes 786432 | tf_op jit(solution)/shard_map/all_to_all | solution.py:52
  39.9 13.6 %copy-start.1 = (f32[2,8]{1,0:T(2,128)S(1)}, f32[2,8]{1,0:T(2,128)}, u32[]{:S(2)}) copy-start(f32[2,8]{1,0:T(2,128)} %param.8) | copy-start | bytes 196
  41.5 51.3 %all-to-all-start.1 = ((bf16[16,10,2,1281]{3,2,1,0:T(2,128)(2,1)}), bf16[16,10,2,1281]{3,2,1,0:T(2,128)(2,1)S(1)}, u32[]{:S(2)}, u32[]{:S(2)}) async-start(bf16[16,10,2,1281]{3,2,1,0:T(2,128)(2,1)} %bitcast.59), calls=%async_computation.1 | async-start | bytes 1802240 | tf_op jit(solution)/shard_map/all_to_all | solution.py:60
  129.0 31.1 %all-to-all-start.2 = ((bf16[64,24,80]{2,1,0:T(8,128)(2,1)}), bf16[64,24,80]{2,1,0:T(8,128)(2,1)S(1)}, u32[]{:S(2)}, u32[]{:S(2)}) async-start(bf16[64,24,80]{2,1,0:T(8,128)(2,1)} %copy.73), calls=%async_computation.2 | async-start | bytes 786432 | tf_op jit(solution)/shard_map/all_to_all | solution.py:76

commit v2 on v1

--- a/solution.py
+++ b/solution.py
@@ -53,11 +53,23 @@
     received = received.reshape(2, MODES, 2, 2, 2, HALF, band_loops)[:, :, :, :, :, :SLOTS]
     lowest = lax.dynamic_slice_in_dim(owner_table, wave_index * SLOTS, SLOTS, 0)
     degree, factors = pair_layout(lowest)
-    partial_sums = jnp.einsum(
-        "hkfrtsj,sjn,htsn->krsfn", received, legendre, factors.astype(jnp.bfloat16),
-        preferred_element_type=jnp.float32,
-    ).astype(jnp.bfloat16).reshape(2 * MODES, SLOTS, 2, NP)
-    bands = lax.all_to_all(partial_sums, "lat", split_axis=0, concat_axis=0, tiled=True)
+    parity = lat_index % 2
+    signs = factors.astype(jnp.bfloat16)
+    away = lax.dynamic_index_in_dim(received, 1 - parity, 3, keepdims=False)
+    kept = lax.dynamic_index_in_dim(received, parity, 3, keepdims=False)
+    passed = jnp.einsum(
+        "hkftsj,sjn,htsn->ksfn", away, legendre, signs, preferred_element_type=jnp.float32
+    ).astype(jnp.bfloat16)
+    n_lat = MODES * 2
+    from_below = lax.ppermute(passed[: MODES // 2], "lat", [(i, (i + 1) % n_lat) for i in range(n_lat)])
+    from_above = lax.ppermute(passed[MODES // 2 :], "lat", [((i + 1) % n_lat, i) for i in range(n_lat)])
+    own = jnp.einsum(
+        "hkftsj,sjn,htsn->ksfn", kept, legendre, signs, preferred_element_type=jnp.float32
+    )
+    merged = jnp.concatenate([own[: MODES // 2] + from_below.astype(jnp.float32),
+                              own[MODES // 2 :] + from_above.astype(jnp.float32)], axis=0).astype(jnp.bfloat16)
+    same_parity = [list(range(0, n_lat, 2)), list(range(1, n_lat, 2))]
+    bands = lax.all_to_all(merged, "lat", split_axis=0, concat_axis=0, tiled=True, axis_index_groups=same_parity)
     raw = jnp.sum(bands.astype(jnp.float32), axis=0)
     mode = lat_index // 2
     divergence, geopotential = implicit_solve(

time: 163 us -> 156 us (0.957)
  waiting for transfers between devices: 62.5 us -> 46.2 us
  starting transfers between devices: 46.6 us -> 51.5 us
  blocking collectives: 31.2 us -> 35 us
    all_to_all x1, waiting for transfers between devices: 36.8 us -> 16.7 us  [body(): lax.all_to_all(merged, 'lat', split_axis=0, concat_axis=0, tiled=True, ax...]
    ppermute x0 -> x2, starting transfers between devices: none -> 13.2 us  [the longest x1 11.3 us: body(): lax.ppermute(passed[MODES // 2:], 'lat', [((i + 1) % n_lat, i) for i in r...]
    all_to_all x1, starting transfers between devices: 11.9 us -> 5.53 us  [body(): lax.all_to_all(merged, 'lat', split_axis=0, concat_axis=0, tiled=True, ax...]
    ppermute x0 -> x2, waiting for transfers between devices: none -> 3.81 us  [the longest x1 2.9 us: body(): lax.ppermute(passed[:MODES // 2], 'lat', [(i, (i + 1) % n_lat) for i in r...]
    all_gather x1, blocking collectives: 31.2 us -> 35 us  [body(): gathered = lax.all_gather(half, 'lat', axis=0, tiled=True)]
    all_to_all x1, starting transfers between devices: 16.5 us -> 14.6 us  [body(): lax.all_to_all(synthesis, 'wave', split_axis=0, concat_axis=0, tiled=True)]
  transfers between devices with their start and end apart: 3 -> 5, of which waited for: 3 -> 5; matrix products, arithmetic and copies ran while one was open for 2% -> 3% of each run, Pallas kernels for 0% -> 0%
where the time goes in v2:
time: 156 us; the launch traced here: 155 us
  starting transfers between devices  51.5 us (33%)
  waiting for transfers between devices  46.2 us (30%)
  blocking collectives  35 us (22%)
  matrix products  7.54 us (5%)
  local copies, waits for them, and re-layouts  6.84 us (4%)
  other arithmetic  5.59 us (4%)
  between operations  2.87 us (2%)
    all_gather x1, blocking collectives, body(): gathered = lax.all_gather(half, 'lat', axis=0, tiled=True)  35 us
    all_to_all x1, starting transfers between devices, body(): lax.all_to_all(ordered, 'wave', split_axis=0, concat_axis=0, tiled=True)  18.2 us
    all_to_all x1, waiting for transfers between devices, body(): lax.all_to_all(merged, 'lat', split_axis=0, concat_axis=0, tiled=True, ax...  16.7 us
    all_to_all x1, starting transfers between devices, body(): lax.all_to_all(synthesis, 'wave', split_axis=0, concat_axis=0, tiled=True)  14.6 us
    all_to_all x1, waiting for transfers between devices, body(): lax.all_to_all(ordered, 'wave', split_axis=0, concat_axis=0, tiled=True)  12.9 us
    all_to_all x1, waiting for transfers between devices, body(): lax.all_to_all(synthesis, 'wave', split_axis=0, concat_axis=0, tiled=True)  12.7 us
    ppermute x1, starting transfers between devices, body(): lax.ppermute(passed[MODES // 2:], 'lat', [((i + 1) % n_lat, i) for i in r...  11.3 us
    all_to_all x1, starting transfers between devices, body(): lax.all_to_all(merged, 'lat', split_axis=0, concat_axis=0, tiled=True, ax...  5.53 us
  transfers between devices with their start and end apart: 5, of which 5 were waited for; matrix products, arithmetic and copies ran while one was open for 3% of the time, Pallas kernels for 0%

profile of v2, /device:TPU:1, one launch (start us, length us, event | category | flops | bytes accessed | tf_op | source)
XLA Modules:
  0.0 155.5 jit_solution(15669491876258876765)
XLA Ops:
  0.6 0.0 copy-start
  0.7 1.0 reshape.626
  1.6 0.1 pad_add_fusion
  1.7 0.1 eq.19
  1.8 2.8 %fusion.8 = bf16[1536,80]{0,1:T(8,128)(2,1)S(1)} fusion(s32[1536]{0:T(1024)S(1)} %eq.19, bf16[1,80,1280]{2,1,0:T(8,128)(2,1)} %param.5, f32[80]{0:T(128)} %param.7, s32[80]{0:T(128)S(1)} %multiply_add_fusion), kind=kOutput, calls=%fused_computation.11 | convolution fusion | flops 317173760 | bytes 457344 | tf_op jit(solution)/shard_map/dot_general | solution.py:49
  4.6 0.9 copy.86
  5.5 18.2 %all-to-all-start = ((bf16[64,24,80]{2,1,0:T(8,128)(2,1)}), bf16[64,24,80]{2,1,0:T(8,128)(2,1)S(1)}, u32[]{:S(2)}, u32[]{:S(2)}) async-start(bf16[64,24,80]{2,1,0:T(8,128)(2,1)} %bitcast.5), calls=%async_computation | async-start | bytes 786432 | tf_op jit(solution)/shard_map/all_to_all | solution.py:52
  23.7 0.8 broadcast_subtract_fusion
  24.5 0.2 iota_compare_fusion.12
  24.7 0.4 fusion.42
  25.1 0.1 add_convert_fusion
  25.2 0.1 stack.23
  25.3 0.1 bitcast_convert_fusion
  25.4 12.9 %all-to-all-done = bf16[64,24,80]{2,1,0:T(8,128)(2,1)S(1)} async-done(((bf16[64,24,80]{2,1,0:T(8,128)(2,1)}), bf16[64,24,80]{2,1,0:T(8,128)(2,1)S(1)}, u32[]{:S(2)}, u32[]{:S(2)}) %all-to-all-start) | async-done | bytes 245792 | tf_op jit(solution)/shard_map/all_to_all | solution.py:52
  38.4 0.1 copy.87
  38.5 0.3 slice.28
  38.7 0.7 constant_dynamic-slice_fusion.1
  39.4 0.0 copy-done
  39.5 0.6 fusion.4
  40.1 0.1 fusion.51
  40.3 1.9 %collective-permute-start = (bf16[4,10,2,1281]{3,0,2,1:T(4,128)(2,1)S(1)}, bf16[4,10,2,1281]{3,0,2,1:T(4,128)(2,1)S(1)}, u32[]{:S(2)}, u32[]{:S(2)}) collective-permute-start(bf16[4,10,2,1281]{3,0,2,1:T(4,128)(2,1)S(1)} %get-tuple-element.16), channel_id=1, source_target_pairs={{0,64},{64,128},{128,192},{192,256},{256,320},{320,384},{384,448},... | collective-permute-start | bytes 614888 | tf_op jit(solution)/shard_map/ppermute | solution.py:64
  42.2 11.3 %collective-permute-start.1 = (bf16[4,10,2,1281]{3,0,2,1:T(4,128)(2,1)S(1)}, bf16[4,10,2,1281]{3,0,2,1:T(4,128)(2,1)S(1)}, u32[]{:S(2)}, u32[]{:S(2)}) collective-permute-start(bf16[4,10,2,1281]{3,0,2,1:T(4,128)(2,1)S(1)} %get-tuple-element.17), channel_id=1, source_target_pairs={{64,0},{128,64},{192,128},{256,192},{320,256},{384,320},{448,384},... | collective-permute-start | bytes 614888 | tf_op jit(solution)/shard_map/ppermute | solution.py:65
  53.5 0.6 fusion.5
  54.1 2.9 %collective-permute-done = bf16[4,10,2,1281]{3,0,2,1:T(4,128)(2,1)S(1)} collective-permute-done((bf16[4,10,2,1281]{3,0,2,1:T(4,128)(2,1)S(1)}, bf16[4,10,2,1281]{3,0,2,1:T(4,128)(2,1)S(1)}, u32[]{:S(2)}, u32[]{:S(2)}) %collective-permute-start) | collective-permute-done | bytes 204992 | tf_op jit(solution)/shard_map/ppermute | solution.py:64
  57.0 0.9 collective-permute-done.1
  57.9 0.0 copy-start.1
  57.9 0.3 fusion.28
  58.2 0.2 pad_maximum_fusion
  58.4 1.1 copy.92
  59.6 5.5 %all-to-all-start.1 = ((bf16[8,10,2,1281]{3,2,1,0:T(2,128)(2,1)}), bf16[8,10,2,1281]{3,2,1,0:T(2,128)(2,1)S(1)}, u32[]{:S(2)}, u32[]{:S(2)}) async-start(bf16[8,10,2,1281]{3,2,1,0:T(2,128)(2,1)} %copy.92), calls=%async_computation.1 | async-start | bytes 901120 | tf_op jit(solution)/shard_map/all_to_all | solution.py:72
  65.1 0.0 copy-done.1
  65.1 0.6 constant_dynamic-slice_fusion
  67.6 16.7 %all-to-all-done.1 = bf16[8,10,2,1281]{3,2,1,0:T(2,128)(2,1)S(1)} async-done(((bf16[8,10,2,1281]{3,2,1,0:T(2,128)(2,1)}), bf16[8,10,2,1281]{3,2,1,0:T(2,128)(2,1)S(1)}, u32[]{:S(2)}, u32[]{:S(2)}) %all-to-all-start.1) | async-done | bytes 409952 | tf_op jit(solution)/shard_map/all_to_all | solution.py:72
  84.4 0.4 convert_reduce_fusion
  84.8 0.4 fusion.49
  85.2 0.7 subtract_convert_fusion
  86.0 35.0 %all_gather.3 = bf16[16,10,2,1281]{3,2,1,0:T(2,128)(2,1)S(1)} all-gather(bf16[1,10,2,1281]{3,2,1,0:T(2,128)(2,1)S(1)} %copy.93), channel_id=1, replica_groups=mesh['lat'=16,'wave'=64] {'lat'}, dimensions={0}, use_global_device_ids=true | all-gather | bytes 871080 | tf_op jit(solution)/shard_map/all_gather | solution.py:80
  121.0 0.1 copy.94
  121.1 1.1 fusion.22
  122.2 0.3 copy.118
  122.6 0.4 pad.10.clone
  123.0 1.0 copy.96
  124.0 14.6 %all-to-all-start.2 = ((bf16[64,24,80]{2,1,0:T(8,128)(2,1)}), bf16[64,24,80]{2,1,0:T(8,128)(2,1)S(1)}, u32[]{:S(2)}, u32[]{:S(2)}) async-start(bf16[64,24,80]{2,1,0:T(8,128)(2,1)} %copy.96), calls=%async_computation.2 | async-start | bytes 786432 | tf_op jit(solution)/shard_map/all_to_all | solution.py:88
  138.6 1.1 bitcast_subtract_fusion
  139.6 0.8 maximum_bitcast_fusion
  140.4 12.7 %all-to-all-done.2 = bf16[64,24,80]{2,1,0:T(8,128)(2,1)S(1)} async-done(((bf16[64,24,80]{2,1,0:T(8,128)(2,1)}), bf16[64,24,80]{2,1,0:T(8,128)(2,1)S(1)}, u32[]{:S(2)}, u32[]{:S(2)}) %all-to-all-start.2) | async-done | bytes 245792 | tf_op jit(solution)/shard_map/all_to_all | solution.py:88
  153.1 2.3 %fusion.11 = bf16[1,80,1280]{2,1,0:T(8,128)(2,1)} fusion(bf16[1536,80]{1,0:T(8,128)(2,1)S(1)} %bitcast.85, s32[1536]{0:T(1024)S(1)} %eq.19, s32[80]{0:T(128)S(1)} %multiply_add_fusion), kind=kOutput, calls=%fused_computation.14 | convolution fusion | flops 316846080 | bytes 457024 | tf_op jit(solution)/shard_map/dot_general | solution.py:89
  (7 shorter events, 0.1 us)
Async XLA Ops:
  0.6 38.8 %copy-start = (bf16[10,80,1281]{2,1,0:T(8,128)(2,1)S(1)}, bf16[10,80,1281]{2,1,0:T(8,128)(2,1)}, u32[]{:S(2)}) copy-start(bf16[10,80,1281]{2,1,0:T(8,128)(2,1)} %param.6) | copy-start | bytes 6148804
  5.5 32.8 %all-to-all-start = ((bf16[64,24,80]{2,1,0:T(8,128)(2,1)}), bf16[64,24,80]{2,1,0:T(8,128)(2,1)S(1)}, u32[]{:S(2)}, u32[]{:S(2)}) async-start(bf16[64,24,80]{2,1,0:T(8,128)(2,1)} %bitcast.5), calls=%async_computation | async-start | bytes 786432 | tf_op jit(solution)/shard_map/all_to_all | solution.py:52
  40.3 16.8 %collective-permute-start = (bf16[4,10,2,1281]{3,0,2,1:T(4,128)(2,1)S(1)}, bf16[4,10,2,1281]{3,0,2,1:T(4,128)(2,1)S(1)}, u32[]{:S(2)}, u32[]{:S(2)}) collective-permute-start(bf16[4,10,2,1281]{3,0,2,1:T(4,128)(2,1)S(1)} %get-tuple-element.16), channel_id=1, source_target_pairs={{0,64},{64,128},{128,192},{192,256},{256,320},{320,384},{384,448},... | collective-permute-start | bytes 614888 | tf_op jit(solution)/shard_map/ppermute | solution.py:64
  42.2 15.7 %collective-permute-start.1 = (bf16[4,10,2,1281]{3,0,2,1:T(4,128)(2,1)S(1)}, bf16[4,10,2,1281]{3,0,2,1:T(4,128)(2,1)S(1)}, u32[]{:S(2)}, u32[]{:S(2)}) collective-permute-start(bf16[4,10,2,1281]{3,0,2,1:T(4,128)(2,1)S(1)} %get-tuple-element.17), channel_id=1, source_target_pairs={{64,0},{128,64},{192,128},{256,192},{320,256},{384,320},{448,384},... | collective-permute-start | bytes 614888 | tf_op jit(solution)/shard_map/ppermute | solution.py:65
  57.9 7.2 %copy-start.1 = (f32[2,8]{1,0:T(2,128)S(1)}, f32[2,8]{1,0:T(2,128)}, u32[]{:S(2)}) copy-start(f32[2,8]{1,0:T(2,128)} %param.8) | copy-start | bytes 196
  59.6 24.8 %all-to-all-start.1 = ((bf16[8,10,2,1281]{3,2,1,0:T(2,128)(2,1)}), bf16[8,10,2,1281]{3,2,1,0:T(2,128)(2,1)S(1)}, u32[]{:S(2)}, u32[]{:S(2)}) async-start(bf16[8,10,2,1281]{3,2,1,0:T(2,128)(2,1)} %copy.92), calls=%async_computation.1 | async-start | bytes 901120 | tf_op jit(solution)/shard_map/all_to_all | solution.py:72
  124.0 29.2 %all-to-all-start.2 = ((bf16[64,24,80]{2,1,0:T(8,128)(2,1)}), bf16[64,24,80]{2,1,0:T(8,128)(2,1)S(1)}, u32[]{:S(2)}, u32[]{:S(2)}) async-start(bf16[64,24,80]{2,1,0:T(8,128)(2,1)} %copy.96), calls=%async_computation.2 | async-start | bytes 786432 | tf_op jit(solution)/shard_map/all_to_all | solution.py:88

commit v3 on v2

--- a/solution.py
+++ b/solution.py
@@ -11,7 +11,6 @@
 CHANNELS = 16
 WAVE = 64
 SLOTS = 10
-HALF = 12
 
 
 def pair_layout(lowest):
@@ -43,14 +42,14 @@
     weighted = jnp.where(
         carried, fourier_in[0].astype(jnp.float32) * quad_weights[:, None], 0.0
     ).astype(jnp.bfloat16)
-    low = jnp.pad(owner_table.reshape(WAVE, SLOTS), ((0, 0), (0, HALF - SLOTS)), constant_values=-1)
-    order = jnp.concatenate([low, jnp.where(low < 0, -1, TRUNC - low)], axis=1).reshape(-1)
+    low = owner_table.reshape(WAVE, SLOTS)
+    order = jnp.concatenate([low, TRUNC - low], axis=1).reshape(-1)
     select = (order[:, None] == wavenumber[None, :]).astype(jnp.bfloat16)
     ordered = lax.dot_general(
         select, weighted, (((1,), (1,)), ((), ())), preferred_element_type=jnp.float32
-    ).astype(jnp.bfloat16).reshape(WAVE, 2 * HALF, band_loops)
+    ).astype(jnp.bfloat16).reshape(WAVE, SLOTS, 2, band_loops)
     received = lax.all_to_all(ordered, "wave", split_axis=0, concat_axis=0, tiled=True)
-    received = received.reshape(2, MODES, 2, 2, 2, HALF, band_loops)[:, :, :, :, :, :SLOTS]
+    received = received.reshape(2, MODES, 2, 2, 2, SLOTS, band_loops)
     lowest = lax.dynamic_slice_in_dim(owner_table, wave_index * SLOTS, SLOTS, 0)
     degree, factors = pair_layout(lowest)
     parity = lat_index % 2
@@ -83,11 +82,10 @@
     synthesis = jnp.einsum(
         "htkfrsn,sjn->hkfrtsj", signed, legendre, preferred_element_type=jnp.float32
     ).astype(jnp.bfloat16)
-    synthesis = jnp.pad(synthesis, ((0, 0),) * 5 + ((0, HALF - SLOTS), (0, 0)))
-    synthesis = synthesis.reshape(WAVE, 2 * HALF, band_loops)
+    synthesis = synthesis.reshape(WAVE, SLOTS, 2, band_loops)
     arrived = lax.all_to_all(synthesis, "wave", split_axis=0, concat_axis=0, tiled=True)
     fourier_out = lax.dot_general(
-        arrived.reshape(WAVE * 2 * HALF, band_loops), select, (((0,), (0,)), ((), ())),
+        arrived.reshape(M, band_loops), select, (((0,), (0,)), ((), ())),
         preferred_element_type=jnp.float32,
     ).astype(jnp.bfloat16)
     fourier_out = jnp.where(carried, fourier_out, jnp.zeros_like(fourier_out))[None]

time: 156 us -> 152 us (0.974)
  waiting for transfers between devices: 46.2 us -> 43.6 us
where the time goes in v3:
time: 152 us
  starting transfers between devices  51.3 us (34%)
  waiting for transfers between devices  43.6 us (29%)
  blocking collectives  35 us (23%)
  matrix products  7.1 us (5%)
  local copies, waits for them, and re-layouts  6.2 us (4%)
  other arithmetic  5.58 us (4%)
  between operations  2.87 us (2%)
    all_gather x1, blocking collectives, body(): gathered = lax.all_gather(half, 'lat', axis=0, tiled=True)  35 us
    all_to_all x1, starting transfers between devices, body(): lax.all_to_all(ordered, 'wave', split_axis=0, concat_axis=0, tiled=True)  18.2 us
    all_to_all x1, waiting for transfers between devices, body(): lax.all_to_all(merged, 'lat', split_axis=0, concat_axis=0, tiled=True, ax...  16.7 us
    all_to_all x1, starting transfers between devices, body(): lax.all_to_all(synthesis, 'wave', split_axis=0, concat_axis=0, tiled=True)  14.4 us
    all_to_all x1, waiting for transfers between devices, body(): lax.all_to_all(ordered, 'wave', split_axis=0, concat_axis=0, tiled=True)  11.6 us
    all_to_all x1, waiting for transfers between devices, body(): lax.all_to_all(synthesis, 'wave', split_axis=0, concat_axis=0, tiled=True)  11.5 us
    ppermute x1, starting transfers between devices, body(): lax.ppermute(passed[MODES // 2:], 'lat', [((i + 1) % n_lat, i) for i in r...  11.3 us
    all_to_all x1, starting transfers between devices, body(): lax.all_to_all(merged, 'lat', split_axis=0, concat_axis=0, tiled=True, ax...  5.53 us
  transfers between devices with their start and end apart: 5, of which 5 were waited for; matrix products, arithmetic and copies ran while one was open for 3% of the time, Pallas kernels for 0%

profile of v3, /device:TPU:1, one launch (start us, length us, event | category | flops | bytes accessed | tf_op | source)
XLA Modules:
  0.0 151.6 jit_solution(7706503339838966861)
XLA Ops:
  0.6 0.0 copy-start
  0.7 1.0 reshape.626
  1.6 0.1 pad_add_fusion
  1.7 0.1 eq.19
  1.8 2.5 %fusion.8 = bf16[1280,80]{0,1:T(8,128)(2,1)S(1)} fusion(s32[1280]{0:T(1024)S(1)} %eq.19, bf16[1,80,1280]{2,1,0:T(8,128)(2,1)} %param.5, f32[80]{0:T(128)} %param.7, s32[80]{0:T(128)S(1)} %multiply_add_fusion), kind=kOutput, calls=%fused_computation.11 | convolution fusion | flops 264396800 | bytes 415360 | tf_op jit(solution)/shard_map/dot_general | solution.py:48
  4.3 0.9 copy.86
  5.2 18.2 %all-to-all-start = ((bf16[64,10,2,80]{3,2,1,0:T(2,128)(2,1)}), bf16[64,10,2,80]{3,2,1,0:T(2,128)(2,1)S(1)}, u32[]{:S(2)}, u32[]{:S(2)}) async-start(bf16[64,10,2,80]{3,2,1,0:T(2,128)(2,1)} %bitcast.5), calls=%async_computation | async-start | bytes 655360 | tf_op jit(solution)/shard_map/all_to_all | solution.py:51
  23.5 0.8 broadcast_subtract_fusion.1
  24.2 0.2 iota_compare_fusion.12
  24.4 0.1 add_convert_fusion
  24.6 0.4 fusion.42
  24.9 0.1 stack.23
  25.0 0.1 bitcast_convert_fusion
  25.2 11.6 %all-to-all-done = bf16[64,10,2,80]{3,2,1,0:T(2,128)(2,1)S(1)} async-done(((bf16[64,10,2,80]{3,2,1,0:T(2,128)(2,1)}), bf16[64,10,2,80]{3,2,1,0:T(2,128)(2,1)S(1)}, u32[]{:S(2)}, u32[]{:S(2)}) %all-to-all-start) | async-done | bytes 204832 | tf_op jit(solution)/shard_map/all_to_all | solution.py:51
  36.8 0.1 copy.87
  36.9 0.7 constant_dynamic-slice_fusion.1
  37.6 0.0 copy-done
  37.6 0.6 fusion.2
  38.2 0.1 fusion.51
  38.4 1.9 %collective-permute-start = (bf16[4,10,2,1281]{3,0,2,1:T(4,128)(2,1)S(1)}, bf16[4,10,2,1281]{3,0,2,1:T(4,128)(2,1)S(1)}, u32[]{:S(2)}, u32[]{:S(2)}) collective-permute-start(bf16[4,10,2,1281]{3,0,2,1:T(4,128)(2,1)S(1)} %get-tuple-element.16), channel_id=1, source_target_pairs={{0,64},{64,128},{128,192},{192,256},{256,320},{320,384},{384,448},... | collective-permute-start | bytes 614888 | tf_op jit(solution)/shard_map/ppermute | solution.py:63
  40.3 11.3 %collective-permute-start.1 = (bf16[4,10,2,1281]{3,0,2,1:T(4,128)(2,1)S(1)}, bf16[4,10,2,1281]{3,0,2,1:T(4,128)(2,1)S(1)}, u32[]{:S(2)}, u32[]{:S(2)}) collective-permute-start(bf16[4,10,2,1281]{3,0,2,1:T(4,128)(2,1)S(1)} %get-tuple-element.17), channel_id=1, source_target_pairs={{64,0},{128,64},{192,128},{256,192},{320,256},{384,320},{448,384},... | collective-permute-start | bytes 614888 | tf_op jit(solution)/shard_map/ppermute | solution.py:64
  51.6 0.6 fusion.3
  52.2 2.9 %collective-permute-done = bf16[4,10,2,1281]{3,0,2,1:T(4,128)(2,1)S(1)} collective-permute-done((bf16[4,10,2,1281]{3,0,2,1:T(4,128)(2,1)S(1)}, bf16[4,10,2,1281]{3,0,2,1:T(4,128)(2,1)S(1)}, u32[]{:S(2)}, u32[]{:S(2)}) %collective-permute-start) | collective-permute-done | bytes 204992 | tf_op jit(solution)/shard_map/ppermute | solution.py:63
  55.1 0.9 collective-permute-done.1
  56.0 0.0 copy-start.1
  56.0 0.3 fusion.28
  56.3 0.2 pad_maximum_fusion
  56.6 1.1 copy.92
  57.7 5.5 %all-to-all-start.1 = ((bf16[8,10,2,1281]{3,2,1,0:T(2,128)(2,1)}), bf16[8,10,2,1281]{3,2,1,0:T(2,128)(2,1)S(1)}, u32[]{:S(2)}, u32[]{:S(2)}) async-start(bf16[8,10,2,1281]{3,2,1,0:T(2,128)(2,1)} %copy.92), calls=%async_computation.1 | async-start | bytes 901120 | tf_op jit(solution)/shard_map/all_to_all | solution.py:71
  63.2 0.0 copy-done.1
  63.2 0.6 constant_dynamic-slice_fusion
  65.8 16.7 %all-to-all-done.1 = bf16[8,10,2,1281]{3,2,1,0:T(2,128)(2,1)S(1)} async-done(((bf16[8,10,2,1281]{3,2,1,0:T(2,128)(2,1)}), bf16[8,10,2,1281]{3,2,1,0:T(2,128)(2,1)S(1)}, u32[]{:S(2)}, u32[]{:S(2)}) %all-to-all-start.1) | async-done | bytes 409952 | tf_op jit(solution)/shard_map/all_to_all | solution.py:71
  82.5 0.4 convert_reduce_fusion
  82.9 0.4 fusion.49
  83.3 0.7 subtract_convert_fusion
  84.2 35.0 %all_gather.3 = bf16[16,10,2,1281]{3,2,1,0:T(2,128)(2,1)S(1)} all-gather(bf16[1,10,2,1281]{3,2,1,0:T(2,128)(2,1)S(1)} %copy.93), channel_id=1, replica_groups=mesh['lat'=16,'wave'=64] {'lat'}, dimensions={0}, use_global_device_ids=true | all-gather | bytes 871080 | tf_op jit(solution)/shard_map/all_gather | solution.py:79
  119.1 0.1 copy.94
  119.2 1.1 fusion.22
  120.4 0.3 copy.95
  120.7 1.1 copy.96
  121.8 14.4 %all-to-all-start.2 = ((bf16[64,10,2,80]{3,2,1,0:T(2,128)(2,1)}), bf16[64,10,2,80]{3,2,1,0:T(2,128)(2,1)S(1)}, u32[]{:S(2)}, u32[]{:S(2)}) async-start(bf16[64,10,2,80]{3,2,1,0:T(2,128)(2,1)} %copy.96), calls=%async_computation.2 | async-start | bytes 655360 | tf_op jit(solution)/shard_map/all_to_all | solution.py:86
  136.2 1.1 bitcast_subtract_fusion
  137.3 0.8 maximum_bitcast_fusion
  138.0 11.5 %all-to-all-done.2 = bf16[64,10,2,80]{3,2,1,0:T(2,128)(2,1)S(1)} async-done(((bf16[64,10,2,80]{3,2,1,0:T(2,128)(2,1)}), bf16[64,10,2,80]{3,2,1,0:T(2,128)(2,1)S(1)}, u32[]{:S(2)}, u32[]{:S(2)}) %all-to-all-start.2) | async-done | bytes 204832 | tf_op jit(solution)/shard_map/all_to_all | solution.py:86
  149.5 2.2 %fusion.11 = bf16[1,80,1280]{2,1,0:T(8,128)(2,1)} fusion(bf16[1280,80]{1,0:T(8,128)(2,1)S(1)} %bitcast.85, s32[1280]{0:T(1024)S(1)} %eq.19, s32[80]{0:T(128)S(1)} %multiply_add_fusion), kind=kOutput, calls=%fused_computation.14 | convolution fusion | flops 264089600 | bytes 415040 | tf_op jit(solution)/shard_map/dot_general | solution.py:87
  (7 shorter events, 0.1 us)
Async XLA Ops:
  0.6 36.9 %copy-start = (bf16[10,80,1281]{2,1,0:T(8,128)(2,1)S(1)}, bf16[10,80,1281]{2,1,0:T(8,128)(2,1)}, u32[]{:S(2)}) copy-start(bf16[10,80,1281]{2,1,0:T(8,128)(2,1)} %param.6) | copy-start | bytes 6148804
  5.2 31.6 %all-to-all-start = ((bf16[64,10,2,80]{3,2,1,0:T(2,128)(2,1)}), bf16[64,10,2,80]{3,2,1,0:T(2,128)(2,1)S(1)}, u32[]{:S(2)}, u32[]{:S(2)}) async-start(bf16[64,10,2,80]{3,2,1,0:T(2,128)(2,1)} %bitcast.5), calls=%async_computation | async-start | bytes 655360 | tf_op jit(solution)/shard_map/all_to_all | solution.py:51
  38.4 16.8 %collective-permute-start = (bf16[4,10,2,1281]{3,0,2,1:T(4,128)(2,1)S(1)}, bf16[4,10,2,1281]{3,0,2,1:T(4,128)(2,1)S(1)}, u32[]{:S(2)}, u32[]{:S(2)}) collective-permute-start(bf16[4,10,2,1281]{3,0,2,1:T(4,128)(2,1)S(1)} %get-tuple-element.16), channel_id=1, source_target_pairs={{0,64},{64,128},{128,192},{192,256},{256,320},{320,384},{384,448},... | collective-permute-start | bytes 614888 | tf_op jit(solution)/shard_map/ppermute | solution.py:63
  40.3 15.7 %collective-permute-start.1 = (bf16[4,10,2,1281]{3,0,2,1:T(4,128)(2,1)S(1)}, bf16[4,10,2,1281]{3,0,2,1:T(4,128)(2,1)S(1)}, u32[]{:S(2)}, u32[]{:S(2)}) collective-permute-start(bf16[4,10,2,1281]{3,0,2,1:T(4,128)(2,1)S(1)} %get-tuple-element.17), channel_id=1, source_target_pairs={{64,0},{128,64},{192,128},{256,192},{320,256},{384,320},{448,384},... | collective-permute-start | bytes 614888 | tf_op jit(solution)/shard_map/ppermute | solution.py:64
  56.0 7.2 %copy-start.1 = (f32[2,8]{1,0:T(2,128)S(1)}, f32[2,8]{1,0:T(2,128)}, u32[]{:S(2)}) copy-start(f32[2,8]{1,0:T(2,128)} %param.8) | copy-start | bytes 196
  57.7 24.8 %all-to-all-start.1 = ((bf16[8,10,2,1281]{3,2,1,0:T(2,128)(2,1)}), bf16[8,10,2,1281]{3,2,1,0:T(2,128)(2,1)S(1)}, u32[]{:S(2)}, u32[]{:S(2)}) async-start(bf16[8,10,2,1281]{3,2,1,0:T(2,128)(2,1)} %copy.92), calls=%async_computation.1 | async-start | bytes 901120 | tf_op jit(solution)/shard_map/all_to_all | solution.py:71
  121.8 27.7 %all-to-all-start.2 = ((bf16[64,10,2,80]{3,2,1,0:T(2,128)(2,1)}), bf16[64,10,2,80]{3,2,1,0:T(2,128)(2,1)S(1)}, u32[]{:S(2)}, u32[]{:S(2)}) async-start(bf16[64,10,2,80]{3,2,1,0:T(2,128)(2,1)} %copy.96), calls=%async_computation.2 | async-start | bytes 655360 | tf_op jit(solution)/shard_map/all_to_all | solution.py:86

commit v4 on v3

--- a/solution.py
+++ b/solution.py
@@ -1,6 +1,8 @@
 import jax
 import jax.numpy as jnp
 from jax import lax
+from jax.experimental import pallas as pl
+from jax.experimental.pallas import tpu as pltpu
 from jax.sharding import PartitionSpec as P
 
 TRUNC = 1279
@@ -11,6 +13,8 @@
 CHANNELS = 16
 WAVE = 64
 SLOTS = 10
+LOOPS = 80
+SPLIT = MODES // 2
 
 
 def pair_layout(lowest):
@@ -32,6 +36,39 @@
     return divergence, geopotential
 
 
+def row_orders(owner_ref):
+    row = lax.broadcasted_iota(jnp.int32, (M, 1), 0)
+    upper = row % 2 == 1
+    slot = row // 2
+    lane = lax.broadcasted_iota(jnp.int32, (M, 128), 1)
+    owner = owner_ref[...].astype(jnp.float32)
+    found = jnp.zeros((M, 128), jnp.float32)
+    for chunk in range(PAIRS // 128):
+        found = jnp.where(lane + 128 * chunk == slot, owner[chunk : chunk + 1], found)
+    low = jnp.sum(found, axis=1, keepdims=True)
+    return jnp.where(upper, float(TRUNC) - low, low).astype(jnp.int32)
+
+def one_hot(order):
+    lane = lax.broadcasted_iota(jnp.int32, (M, M), 1)
+    return jnp.where(lane == order, 1.0, 0.0).astype(jnp.bfloat16)
+
+def gather_kernel(lat_ref, fourier_ref, quad_ref, owner_ref, out_ref):
+    order = row_orders(owner_ref)
+    moved = lax.dot_general(one_hot(order), fourier_ref[...], (((1,), (1,)), ((), ())), preferred_element_type=jnp.float32)
+    loop = lat_ref[0] * LOOPS + lax.broadcasted_iota(jnp.int32, (M, LOOPS), 1)
+    out_ref[...] = jnp.where(order <= 2 * loop + 9, moved * quad_ref[...], 0.0).astype(jnp.bfloat16)
+
+def gather_rows(lat, fourier, quad, owner):
+    vm = pl.BlockSpec(memory_space=pltpu.VMEM)
+    return pl.pallas_call(
+        gather_kernel,
+        out_shape=jax.ShapeDtypeStruct((M, LOOPS), jnp.bfloat16),
+        in_specs=[pl.BlockSpec(memory_space=pltpu.SMEM), vm, vm, vm],
+        out_specs=vm,
+        name="gather_rows",
+    )(lat, fourier, quad, owner)
+
+
 def body(fourier_in, legendre, quad_weights, si_coeffs, owner_table):
     lat_index = lax.axis_index("lat")
     wave_index = lax.axis_index("wave")
@@ -39,17 +76,11 @@
     loop_index = lat_index * band_loops + jnp.arange(band_loops, dtype=jnp.int32)
     wavenumber = jnp.arange(M, dtype=jnp.int32)
     carried = wavenumber[None, :] <= 2 * loop_index[:, None] + 9
-    weighted = jnp.where(
-        carried, fourier_in[0].astype(jnp.float32) * quad_weights[:, None], 0.0
-    ).astype(jnp.bfloat16)
-    low = owner_table.reshape(WAVE, SLOTS)
-    order = jnp.concatenate([low, TRUNC - low], axis=1).reshape(-1)
-    select = (order[:, None] == wavenumber[None, :]).astype(jnp.bfloat16)
-    ordered = lax.dot_general(
-        select, weighted, (((1,), (1,)), ((), ())), preferred_element_type=jnp.float32
-    ).astype(jnp.bfloat16).reshape(WAVE, SLOTS, 2, band_loops)
+    ordered = gather_rows(
+        lat_index[None].astype(jnp.int32), fourier_in[0], quad_weights[None], owner_table.reshape(PAIRS // 128, 128)
+    ).reshape(WAVE, SLOTS, 2, band_loops)
     received = lax.all_to_all(ordered, "wave", split_axis=0, concat_axis=0, tiled=True)
-    received = received.reshape(2, MODES, 2, 2, 2, SLOTS, band_loops)
+    received = received.reshape(2, MODES, 2, 2, SLOTS, 2, band_loops)
     lowest = lax.dynamic_slice_in_dim(owner_table, wave_index * SLOTS, SLOTS, 0)
     degree, factors = pair_layout(lowest)
     parity = lat_index % 2
@@ -57,16 +88,16 @@
     away = lax.dynamic_index_in_dim(received, 1 - parity, 3, keepdims=False)
     kept = lax.dynamic_index_in_dim(received, parity, 3, keepdims=False)
     passed = jnp.einsum(
-        "hkftsj,sjn,htsn->ksfn", away, legendre, signs, preferred_element_type=jnp.float32
+        "hkfstj,sjn,htsn->ksfn", away, legendre, signs, preferred_element_type=jnp.float32
     ).astype(jnp.bfloat16)
     n_lat = MODES * 2
-    from_below = lax.ppermute(passed[: MODES // 2], "lat", [(i, (i + 1) % n_lat) for i in range(n_lat)])
-    from_above = lax.ppermute(passed[MODES // 2 :], "lat", [((i + 1) % n_lat, i) for i in range(n_lat)])
+    from_below = lax.ppermute(passed[:SPLIT], "lat", [(i, (i + 1) % n_lat) for i in range(n_lat)])
+    from_above = lax.ppermute(passed[SPLIT:], "lat", [((i + 1) % n_lat, i) for i in range(n_lat)])
     own = jnp.einsum(
-        "hkftsj,sjn,htsn->ksfn", kept, legendre, signs, preferred_element_type=jnp.float32
+        "hkfstj,sjn,htsn->ksfn", kept, legendre, signs, preferred_element_type=jnp.float32
     )
-    merged = jnp.concatenate([own[: MODES // 2] + from_below.astype(jnp.float32),
-                              own[MODES // 2 :] + from_above.astype(jnp.float32)], axis=0).astype(jnp.bfloat16)
+    merged = jnp.concatenate([own[:SPLIT] + from_below.astype(jnp.float32),
+                              own[SPLIT:] + from_above.astype(jnp.float32)], axis=0).astype(jnp.bfloat16)
     same_parity = [list(range(0, n_lat, 2)), list(range(1, n_lat, 2))]
     bands = lax.all_to_all(merged, "lat", split_axis=0, concat_axis=0, tiled=True, axis_index_groups=same_parity)
     raw = jnp.sum(bands.astype(jnp.float32), axis=0)
@@ -80,10 +111,12 @@
     fields = gathered.reshape(MODES, 2, SLOTS, 2, NP)
     signed = factors.astype(jnp.bfloat16)[:, :, None, None, None] * jnp.transpose(fields, (0, 3, 1, 2, 4))[None, None]
     synthesis = jnp.einsum(
-        "htkfrsn,sjn->hkfrtsj", signed, legendre, preferred_element_type=jnp.float32
+        "htkfrsn,sjn->hkfrstj", signed, legendre, preferred_element_type=jnp.float32
     ).astype(jnp.bfloat16)
     synthesis = synthesis.reshape(WAVE, SLOTS, 2, band_loops)
     arrived = lax.all_to_all(synthesis, "wave", split_axis=0, concat_axis=0, tiled=True)
+    order = jnp.stack([owner_table, TRUNC - owner_table], axis=1).reshape(-1)
+    select = (order[:, None] == wavenumber[None, :]).astype(jnp.bfloat16)
     fourier_out = lax.dot_general(
         arrived.reshape(M, band_loops), select, (((0,), (0,)), ((), ())),
         preferred_element_type=jnp.float32,

time: 152 us -> 150 us (0.987)
  Pallas kernels: 0 us -> 2.93 us
  matrix products: 7.1 us -> 4.58 us
  local copies, waits for them, and re-layouts: 6.2 us -> 4.13 us
    pallas_call x0 -> x1, Pallas kernels: none -> 2.93 us  [gather_rows(): pl.pallas_call(gather_kernel, out_shape=jax.ShapeDtypeStruct((M, LOOPS),...]
    dot_general x4 -> x3, matrix products: 4.92 us -> 2.41 us  [the longest x1 1.13 us: body(): jnp.einsum('htkfrsn,sjn->hkfrstj', signed, legendre, preferred_element_ty...]
where the time goes in v4:
time: 150 us; the launch traced here: 149 us
  starting transfers between devices  51.3 us (34%)
  waiting for transfers between devices  43.1 us (29%)
  blocking collectives  35 us (23%)
  other arithmetic  5.45 us (4%)
  matrix products  4.58 us (3%)
  local copies, waits for them, and re-layouts  4.13 us (3%)
  Pallas kernels  2.93 us (2%)
  between operations  2.87 us (2%)
    all_gather x1, blocking collectives, body(): gathered = lax.all_gather(half, 'lat', axis=0, tiled=True)  35 us
    all_to_all x1, starting transfers between devices, body(): lax.all_to_all(ordered, 'wave', split_axis=0, concat_axis=0, tiled=True)  18.2 us
    all_to_all x1, waiting for transfers between devices, body(): lax.all_to_all(merged, 'lat', split_axis=0, concat_axis=0, tiled=True, ax...  16.2 us
    all_to_all x1, starting transfers between devices, body(): lax.all_to_all(synthesis, 'wave', split_axis=0, concat_axis=0, tiled=True)  14.4 us
    all_to_all x1, waiting for transfers between devices, body(): lax.all_to_all(ordered, 'wave', split_axis=0, concat_axis=0, tiled=True)  11.6 us
    all_to_all x1, waiting for transfers between devices, body(): lax.all_to_all(synthesis, 'wave', split_axis=0, concat_axis=0, tiled=True)  11.5 us
    ppermute x1, starting transfers between devices, body(): lax.ppermute(passed[SPLIT:], 'lat', [((i + 1) % n_lat, i) for i in range(...  11.3 us
    all_to_all x1, starting transfers between devices, body(): lax.all_to_all(merged, 'lat', split_axis=0, concat_axis=0, tiled=True, ax...  5.54 us
  transfers between devices with their start and end apart: 5, of which 5 were waited for; matrix products, arithmetic and copies ran while one was open for 3% of the time, Pallas kernels for 0%

profile of v4, /device:TPU:1, one launch (start us, length us, event | category | flops | bytes accessed | tf_op | source)
XLA Modules:
  0.0 149.4 jit_solution(149698839082349043)
XLA Ops:
  0.6 0.0 copy-start
  0.7 2.9 %gather_rows.1 = bf16[1280,80]{1,0:T(8,128)(2,1)} custom-call(s32[1]{0:T(128)} %bitcast.4.lat_ref, bf16[80,1280]{1,0:T(8,128)(2,1)} %bitcast.83, f32[1,80]{1,0:T(1,128)} %bitcast.85, s32[5,128]{1,0:T(8,128)} %bitcast.84), custom_call_target="tpu_custom_call" | custom-call | tf_op jit(solution)/shard_map/gather_rows/pallas_call | solution.py:63
  3.6 18.2 %all-to-all-start = ((bf16[64,10,2,80]{3,2,1,0:T(2,128)(2,1)}), bf16[64,10,2,80]{3,2,1,0:T(2,128)(2,1)S(1)}, u32[]{:S(2)}, u32[]{:S(2)}) async-start(bf16[64,10,2,80]{3,2,1,0:T(2,128)(2,1)} %bitcast.80), calls=%async_computation | async-start | bytes 655360 | tf_op jit(solution)/shard_map/all_to_all | solution.py:82
  21.8 0.8 broadcast_subtract_fusion.1
  22.6 0.2 iota_compare_fusion.9
  22.7 0.1 add_convert_fusion
  22.9 0.4 fusion.28
  23.3 0.1 stack.32
  23.4 0.1 bitcast_convert_fusion
  23.5 11.6 %all-to-all-done = bf16[64,10,2,80]{3,2,1,0:T(2,128)(2,1)S(1)} async-done(((bf16[64,10,2,80]{3,2,1,0:T(2,128)(2,1)}), bf16[64,10,2,80]{3,2,1,0:T(2,128)(2,1)S(1)}, u32[]{:S(2)}, u32[]{:S(2)}) %all-to-all-start) | async-done | bytes 204832 | tf_op jit(solution)/shard_map/all_to_all | solution.py:82
  35.1 0.2 constant_dynamic-slice_fusion.1
  35.4 0.0 copy-done
  35.4 0.6 fusion.1
  36.0 0.1 fusion.36
  36.2 1.9 %collective-permute-start = (bf16[4,10,2,1281]{3,0,2,1:T(4,128)(2,1)S(1)}, bf16[4,10,2,1281]{3,0,2,1:T(4,128)(2,1)S(1)}, u32[]{:S(2)}, u32[]{:S(2)}) collective-permute-start(bf16[4,10,2,1281]{3,0,2,1:T(4,128)(2,1)S(1)} %get-tuple-element.16), channel_id=1, source_target_pairs={{0,64},{64,128},{128,192},{192,256},{256,320},{320,384},{384,448},... | collective-permute-start | bytes 614888 | tf_op jit(solution)/shard_map/ppermute | solution.py:94
  38.1 11.3 %collective-permute-start.1 = (bf16[4,10,2,1281]{3,0,2,1:T(4,128)(2,1)S(1)}, bf16[4,10,2,1281]{3,0,2,1:T(4,128)(2,1)S(1)}, u32[]{:S(2)}, u32[]{:S(2)}) collective-permute-start(bf16[4,10,2,1281]{3,0,2,1:T(4,128)(2,1)S(1)} %get-tuple-element.17), channel_id=1, source_target_pairs={{64,0},{128,64},{192,128},{256,192},{320,256},{384,320},{448,384},... | collective-permute-start | bytes 614888 | tf_op jit(solution)/shard_map/ppermute | solution.py:95
  49.4 0.6 fusion.2
  50.0 2.9 %collective-permute-done = bf16[4,10,2,1281]{3,0,2,1:T(4,128)(2,1)S(1)} collective-permute-done((bf16[4,10,2,1281]{3,0,2,1:T(4,128)(2,1)S(1)}, bf16[4,10,2,1281]{3,0,2,1:T(4,128)(2,1)S(1)}, u32[]{:S(2)}, u32[]{:S(2)}) %collective-permute-start) | collective-permute-done | bytes 204992 | tf_op jit(solution)/shard_map/ppermute | solution.py:94
  52.9 0.9 collective-permute-done.1
  53.8 0.0 copy-start.1
  53.8 0.0 copy-start.2
  53.8 0.3 fusion.25
  54.1 0.2 pad_maximum_fusion
  54.4 1.1 copy.52
  55.5 5.5 %all-to-all-start.1 = ((bf16[8,10,2,1281]{3,2,1,0:T(2,128)(2,1)}), bf16[8,10,2,1281]{3,2,1,0:T(2,128)(2,1)S(1)}, u32[]{:S(2)}, u32[]{:S(2)}) async-start(bf16[8,10,2,1281]{3,2,1,0:T(2,128)(2,1)} %copy.52), calls=%async_computation.1 | async-start | bytes 901120 | tf_op jit(solution)/shard_map/all_to_all | solution.py:102
  61.0 0.0 copy-done.1
  61.1 0.0 copy-done.2
  61.1 0.6 constant_dynamic-slice_fusion
  63.7 0.2 copy.57
  63.8 0.2 eq.19
  64.1 16.2 %all-to-all-done.1 = bf16[8,10,2,1281]{3,2,1,0:T(2,128)(2,1)S(1)} async-done(((bf16[8,10,2,1281]{3,2,1,0:T(2,128)(2,1)}), bf16[8,10,2,1281]{3,2,1,0:T(2,128)(2,1)S(1)}, u32[]{:S(2)}, u32[]{:S(2)}) %all-to-all-start.1) | async-done | bytes 409952 | tf_op jit(solution)/shard_map/all_to_all | solution.py:102
  80.3 0.4 convert_reduce_fusion
  80.7 0.4 fusion.34
  81.1 0.7 subtract_convert_fusion
  81.9 35.0 %all_gather.3 = bf16[16,10,2,1281]{3,2,1,0:T(2,128)(2,1)S(1)} all-gather(bf16[1,10,2,1281]{3,2,1,0:T(2,128)(2,1)S(1)} %copy.53), channel_id=1, replica_groups=mesh['lat'=16,'wave'=64] {'lat'}, dimensions={0}, use_global_device_ids=true | all-gather | bytes 871080 | tf_op jit(solution)/shard_map/all_gather | solution.py:110
  116.9 0.1 copy.54
  117.0 1.1 fusion.19
  118.2 0.3 copy.55
  118.5 1.1 copy.56
  119.6 14.4 %all-to-all-start.2 = ((bf16[64,10,2,80]{3,2,1,0:T(2,128)(2,1)}), bf16[64,10,2,80]{3,2,1,0:T(2,128)(2,1)S(1)}, u32[]{:S(2)}, u32[]{:S(2)}) async-start(bf16[64,10,2,80]{3,2,1,0:T(2,128)(2,1)} %copy.56), calls=%async_computation.2 | async-start | bytes 655360 | tf_op jit(solution)/shard_map/all_to_all | solution.py:117
  134.0 1.0 bitcast_subtract_fusion
  135.0 0.8 maximum_bitcast_fusion
  135.8 11.5 %all-to-all-done.2 = bf16[64,10,2,80]{3,2,1,0:T(2,128)(2,1)S(1)} async-done(((bf16[64,10,2,80]{3,2,1,0:T(2,128)(2,1)}), bf16[64,10,2,80]{3,2,1,0:T(2,128)(2,1)S(1)}, u32[]{:S(2)}, u32[]{:S(2)}) %all-to-all-start.2) | async-done | bytes 204832 | tf_op jit(solution)/shard_map/all_to_all | solution.py:117
  147.3 2.2 %fusion.8 = bf16[1,80,1280]{2,1,0:T(8,128)(2,1)} fusion(bf16[1280,80]{1,0:T(8,128)(2,1)S(1)} %bitcast.82, s32[1280]{0:T(1024)S(1)} %eq.19, s32[80]{0:T(128)S(1)} %multiply_add_fusion), kind=kOutput, calls=%fused_computation.11 | convolution fusion | flops 264089600 | bytes 415040 | tf_op jit(solution)/shard_map/dot_general | solution.py:120
  (10 shorter events, 0.1 us)
Async XLA Ops:
  0.6 34.7 %copy-start = (bf16[10,80,1281]{2,1,0:T(8,128)(2,1)S(1)}, bf16[10,80,1281]{2,1,0:T(8,128)(2,1)}, u32[]{:S(2)}) copy-start(bf16[10,80,1281]{2,1,0:T(8,128)(2,1)} %param.6) | copy-start | bytes 6148804
  3.6 31.6 %all-to-all-start = ((bf16[64,10,2,80]{3,2,1,0:T(2,128)(2,1)}), bf16[64,10,2,80]{3,2,1,0:T(2,128)(2,1)S(1)}, u32[]{:S(2)}, u32[]{:S(2)}) async-start(bf16[64,10,2,80]{3,2,1,0:T(2,128)(2,1)} %bitcast.80), calls=%async_computation | async-start | bytes 655360 | tf_op jit(solution)/shard_map/all_to_all | solution.py:82
  36.2 16.8 %collective-permute-start = (bf16[4,10,2,1281]{3,0,2,1:T(4,128)(2,1)S(1)}, bf16[4,10,2,1281]{3,0,2,1:T(4,128)(2,1)S(1)}, u32[]{:S(2)}, u32[]{:S(2)}) collective-permute-start(bf16[4,10,2,1281]{3,0,2,1:T(4,128)(2,1)S(1)} %get-tuple-element.16), channel_id=1, source_target_pairs={{0,64},{64,128},{128,192},{192,256},{256,320},{320,384},{384,448},... | collective-permute-start | bytes 614888 | tf_op jit(solution)/shard_map/ppermute | solution.py:94
  38.1 15.7 %collective-permute-start.1 = (bf16[4,10,2,1281]{3,0,2,1:T(4,128)(2,1)S(1)}, bf16[4,10,2,1281]{3,0,2,1:T(4,128)(2,1)S(1)}, u32[]{:S(2)}, u32[]{:S(2)}) collective-permute-start(bf16[4,10,2,1281]{3,0,2,1:T(4,128)(2,1)S(1)} %get-tuple-element.17), channel_id=1, source_target_pairs={{64,0},{128,64},{192,128},{256,192},{320,256},{384,320},{448,384},... | collective-permute-start | bytes 614888 | tf_op jit(solution)/shard_map/ppermute | solution.py:95
  53.8 7.2 %copy-start.1 = (s32[640]{0:T(1024)S(1)}, s32[640]{0:T(1024)}, u32[]{:S(2)}) copy-start(s32[640]{0:T(1024)} %param.9) | copy-start | bytes 7684
  53.8 7.2 %copy-start.2 = (f32[2,8]{1,0:T(2,128)S(1)}, f32[2,8]{1,0:T(2,128)}, u32[]{:S(2)}) copy-start(f32[2,8]{1,0:T(2,128)} %param.8) | copy-start | bytes 196
  55.5 24.8 %all-to-all-start.1 = ((bf16[8,10,2,1281]{3,2,1,0:T(2,128)(2,1)}), bf16[8,10,2,1281]{3,2,1,0:T(2,128)(2,1)S(1)}, u32[]{:S(2)}, u32[]{:S(2)}) async-start(bf16[8,10,2,1281]{3,2,1,0:T(2,128)(2,1)} %copy.52), calls=%async_computation.1 | async-start | bytes 901120 | tf_op jit(solution)/shard_map/all_to_all | solution.py:102
  119.6 27.7 %all-to-all-start.2 = ((bf16[64,10,2,80]{3,2,1,0:T(2,128)(2,1)}), bf16[64,10,2,80]{3,2,1,0:T(2,128)(2,1)S(1)}, u32[]{:S(2)}, u32[]{:S(2)}) async-start(bf16[64,10,2,80]{3,2,1,0:T(2,128)(2,1)} %copy.56), calls=%async_computation.2 | async-start | bytes 655360 | tf_op jit(solution)/shard_map/all_to_all | solution.py:117

commit v5 on v4

--- a/solution.py
+++ b/solution.py
@@ -96,8 +96,8 @@
     own = jnp.einsum(
         "hkfstj,sjn,htsn->ksfn", kept, legendre, signs, preferred_element_type=jnp.float32
     )
-    merged = jnp.concatenate([own[:SPLIT] + from_below.astype(jnp.float32),
-                              own[SPLIT:] + from_above.astype(jnp.float32)], axis=0).astype(jnp.bfloat16)
+    incoming = jnp.concatenate([from_below, from_above], axis=0).astype(jnp.float32)
+    merged = (own + incoming).astype(jnp.bfloat16)
     same_parity = [list(range(0, n_lat, 2)), list(range(1, n_lat, 2))]
     bands = lax.all_to_all(merged, "lat", split_axis=0, concat_axis=0, tiled=True, axis_index_groups=same_parity)
     raw = jnp.sum(bands.astype(jnp.float32), axis=0)
@@ -106,7 +106,11 @@
         (raw[:, 0], raw[:, 1]), si_coeffs[0, mode], si_coeffs[1, mode], degree
     )
     spectral = jnp.stack([divergence, geopotential], axis=0)[None]
-    half = jnp.stack([divergence, geopotential], axis=1).astype(jnp.bfloat16)[None]
+    both = implicit_solve(
+        (raw[:, :1], raw[:, 1:]), si_coeffs[0, mode], si_coeffs[1, mode], degree[:, None]
+    )
+    field = jnp.arange(2, dtype=jnp.int32)[None, :, None]
+    half = jnp.where(field == 0, both[0], both[1]).astype(jnp.bfloat16)[None]
     gathered = lax.all_gather(half, "lat", axis=0, tiled=True)
     fields = gathered.reshape(MODES, 2, SLOTS, 2, NP)
     signed = factors.astype(jnp.bfloat16)[:, :, None, None, None] * jnp.transpose(fields, (0, 3, 1, 2, 4))[None, None]

time: 150 us -> 147 us (0.980)
  waiting for transfers between devices: 43.1 us -> 53.6 us
  blocking collectives: 35 us -> 25.5 us
  starting transfers between devices: 51.3 us -> 48 us
    all_gather x1, blocking collectives: 35 us -> 25.5 us  [body(): gathered = lax.all_gather(half, 'lat', axis=0, tiled=True)]
    all_to_all x1, waiting for transfers between devices: 16.2 us -> 23.6 us  [body(): lax.all_to_all(merged, 'lat', split_axis=0, concat_axis=0, tiled=True, ax...]
    ppermute x1, waiting for transfers between devices: 2.9 us -> 5.05 us  [body(): lax.ppermute(passed[:SPLIT], 'lat', [(i, (i + 1) % n_lat) for i in range(...]
    all_to_all x1, starting transfers between devices: 5.54 us -> 3.47 us  [body(): lax.all_to_all(merged, 'lat', split_axis=0, concat_axis=0, tiled=True, ax...]
where the time goes in v5:
time: 147 us
  waiting for transfers between devices  53.6 us (36%)
  starting transfers between devices  48 us (33%)
  blocking collectives  25.5 us (17%)
  other arithmetic  5.19 us (4%)
  matrix products  4.59 us (3%)
  local copies, waits for them, and re-layouts  4.05 us (3%)
  Pallas kernels  2.93 us (2%)
  between operations  2.88 us (2%)
    all_gather x1, blocking collectives, body(): gathered = lax.all_gather(half, 'lat', axis=0, tiled=True)  25.5 us
    all_to_all x1, waiting for transfers between devices, body(): lax.all_to_all(merged, 'lat', split_axis=0, concat_axis=0, tiled=True, ax...  23.6 us
    all_to_all x1, starting transfers between devices, body(): lax.all_to_all(ordered, 'wave', split_axis=0, concat_axis=0, tiled=True)  18.2 us
    all_to_all x1, starting transfers between devices, body(): lax.all_to_all(synthesis, 'wave', split_axis=0, concat_axis=0, tiled=True)  13.2 us
    all_to_all x1, waiting for transfers between devices, body(): lax.all_to_all(ordered, 'wave', split_axis=0, concat_axis=0, tiled=True)  11.6 us
    all_to_all x1, waiting for transfers between devices, body(): lax.all_to_all(synthesis, 'wave', split_axis=0, concat_axis=0, tiled=True)  11.5 us
    ppermute x1, starting transfers between devices, body(): lax.ppermute(passed[SPLIT:], 'lat', [((i + 1) % n_lat, i) for i in range(...  11.3 us
    ppermute x1, waiting for transfers between devices, body(): lax.ppermute(passed[:SPLIT], 'lat', [(i, (i + 1) % n_lat) for i in range(...  5.05 us
  transfers between devices with their start and end apart: 5, of which 5 were waited for; matrix products, arithmetic and copies ran while one was open for 3% of the time, Pallas kernels for 0%

profile of v5, /device:TPU:1, one launch (start us, length us, event | category | flops | bytes accessed | tf_op | source)
XLA Modules:
  0.0 146.8 jit_solution(8355264415250328542)
XLA Ops:
  0.6 0.0 copy-start
  0.7 2.9 %gather_rows.1 = bf16[1280,80]{1,0:T(8,128)(2,1)} custom-call(s32[1]{0:T(128)} %bitcast.4.lat_ref, bf16[80,1280]{1,0:T(8,128)(2,1)} %bitcast.85, f32[1,80]{1,0:T(1,128)} %bitcast.87, s32[5,128]{1,0:T(8,128)} %bitcast.86), custom_call_target="tpu_custom_call" | custom-call | tf_op jit(solution)/shard_map/gather_rows/pallas_call | solution.py:63
  3.6 18.2 %all-to-all-start = ((bf16[64,10,2,80]{3,2,1,0:T(2,128)(2,1)}), bf16[64,10,2,80]{3,2,1,0:T(2,128)(2,1)S(1)}, u32[]{:S(2)}, u32[]{:S(2)}) async-start(bf16[64,10,2,80]{3,2,1,0:T(2,128)(2,1)} %bitcast.82), calls=%async_computation | async-start | bytes 655360 | tf_op jit(solution)/shard_map/all_to_all | solution.py:82
  21.8 0.8 broadcast_subtract_fusion.1
  22.6 0.2 iota_compare_fusion.9
  22.7 0.1 add_convert_fusion
  22.9 0.4 fusion.27
  23.3 0.1 stack.23
  23.4 0.1 bitcast_convert_fusion
  23.5 11.6 %all-to-all-done = bf16[64,10,2,80]{3,2,1,0:T(2,128)(2,1)S(1)} async-done(((bf16[64,10,2,80]{3,2,1,0:T(2,128)(2,1)}), bf16[64,10,2,80]{3,2,1,0:T(2,128)(2,1)S(1)}, u32[]{:S(2)}, u32[]{:S(2)}) %all-to-all-start) | async-done | bytes 204832 | tf_op jit(solution)/shard_map/all_to_all | solution.py:82
  35.1 0.2 constant_dynamic-slice_fusion.1
  35.4 0.0 copy-done
  35.4 0.6 fusion.1
  36.0 0.1 fusion.34
  36.2 11.3 %collective-permute-start.1 = (bf16[4,10,2,1281]{3,0,2,1:T(4,128)(2,1)S(1)}, bf16[4,10,2,1281]{3,0,2,1:T(4,128)(2,1)S(1)}, u32[]{:S(2)}, u32[]{:S(2)}) collective-permute-start(bf16[4,10,2,1281]{3,0,2,1:T(4,128)(2,1)S(1)} %get-tuple-element.11), channel_id=1, source_target_pairs={{64,0},{128,64},{192,128},{256,192},{320,256},{384,320},{448,384},... | collective-permute-start | bytes 614888 | tf_op jit(solution)/shard_map/ppermute | solution.py:95
  47.5 1.9 %collective-permute-start = (bf16[4,10,2,1281]{3,0,2,1:T(4,128)(2,1)S(1)}, bf16[4,10,2,1281]{3,0,2,1:T(4,128)(2,1)S(1)}, u32[]{:S(2)}, u32[]{:S(2)}) collective-permute-start(bf16[4,10,2,1281]{3,0,2,1:T(4,128)(2,1)S(1)} %get-tuple-element.10), channel_id=1, source_target_pairs={{0,64},{64,128},{128,192},{192,256},{256,320},{320,384},{384,448},... | collective-permute-start | bytes 614888 | tf_op jit(solution)/shard_map/ppermute | solution.py:94
  49.4 0.6 fusion.2
  50.0 0.0 copy-start.1
  50.0 0.0 copy-start.2
  50.1 1.8 %collective-permute-done.1 = bf16[4,10,2,1281]{3,0,2,1:T(4,128)(2,1)S(1)} collective-permute-done((bf16[4,10,2,1281]{3,0,2,1:T(4,128)(2,1)S(1)}, bf16[4,10,2,1281]{3,0,2,1:T(4,128)(2,1)S(1)}, u32[]{:S(2)}, u32[]{:S(2)}) %collective-permute-start.1) | collective-permute-done | bytes 204992 | tf_op jit(solution)/shard_map/ppermute | solution.py:95
  51.9 5.0 %collective-permute-done = bf16[4,10,2,1281]{3,0,2,1:T(4,128)(2,1)S(1)} collective-permute-done((bf16[4,10,2,1281]{3,0,2,1:T(4,128)(2,1)S(1)}, bf16[4,10,2,1281]{3,0,2,1:T(4,128)(2,1)S(1)}, u32[]{:S(2)}, u32[]{:S(2)}) %collective-permute-start) | collective-permute-done | bytes 204992 | tf_op jit(solution)/shard_map/ppermute | solution.py:94
  57.0 0.3 fusion.24
  57.2 1.1 copy.25
  58.4 3.5 %all-to-all-start.1 = ((bf16[8,10,2,1281]{3,2,1,0:T(2,128)(2,1)}), bf16[8,10,2,1281]{3,2,1,0:T(2,128)(2,1)S(1)}, u32[]{:S(2)}, u32[]{:S(2)}) async-start(bf16[8,10,2,1281]{3,2,1,0:T(2,128)(2,1)} %copy.25), calls=%async_computation.1 | async-start | bytes 901120 | tf_op jit(solution)/shard_map/all_to_all | solution.py:102
  61.8 0.0 copy-done.1
  61.9 0.0 copy-done.2
  61.9 0.6 constant_dynamic-slice_fusion
  64.4 0.2 copy.29
  64.6 0.2 eq.28
  64.9 23.6 %all-to-all-done.1 = bf16[8,10,2,1281]{3,2,1,0:T(2,128)(2,1)S(1)} async-done(((bf16[8,10,2,1281]{3,2,1,0:T(2,128)(2,1)}), bf16[8,10,2,1281]{3,2,1,0:T(2,128)(2,1)S(1)}, u32[]{:S(2)}, u32[]{:S(2)}) %all-to-all-start.1) | async-done | bytes 409952 | tf_op jit(solution)/shard_map/all_to_all | solution.py:102
  88.5 0.4 convert_reduce_fusion
  88.9 1.0 multiply_subtract_fusion
  89.9 0.1 select_convert_fusion
  90.0 25.5 %all_gather.3 = bf16[16,10,2,1281]{3,2,1,0:T(2,128)(2,1)S(1)} all-gather(bf16[1,10,2,1281]{3,2,1,0:T(2,128)(2,1)S(1)} %select_convert_fusion), channel_id=1, replica_groups=mesh['lat'=16,'wave'=64] {'lat'}, dimensions={0}, use_global_device_ids=true | all-gather | bytes 871080 | tf_op jit(solution)/shard_map/all_gather | solution.py:114
  115.5 0.1 copy.26
  115.6 1.1 fusion.19
  116.8 0.3 copy.27
  117.1 1.1 copy.28
  118.2 13.2 %all-to-all-start.2 = ((bf16[64,10,2,80]{3,2,1,0:T(2,128)(2,1)}), bf16[64,10,2,80]{3,2,1,0:T(2,128)(2,1)S(1)}, u32[]{:S(2)}, u32[]{:S(2)}) async-start(bf16[64,10,2,80]{3,2,1,0:T(2,128)(2,1)} %copy.28), calls=%async_computation.2 | async-start | bytes 655360 | tf_op jit(solution)/shard_map/all_to_all | solution.py:121
  131.4 1.0 bitcast_subtract_fusion
  132.4 0.8 maximum_bitcast_fusion
  133.1 11.5 %all-to-all-done.2 = bf16[64,10,2,80]{3,2,1,0:T(2,128)(2,1)S(1)} async-done(((bf16[64,10,2,80]{3,2,1,0:T(2,128)(2,1)}), bf16[64,10,2,80]{3,2,1,0:T(2,128)(2,1)S(1)}, u32[]{:S(2)}, u32[]{:S(2)}) %all-to-all-start.2) | async-done | bytes 204832 | tf_op jit(solution)/shard_map/all_to_all | solution.py:121
  144.6 2.2 %fusion.8 = bf16[1,80,1280]{2,1,0:T(8,128)(2,1)} fusion(bf16[1280,80]{1,0:T(8,128)(2,1)S(1)} %bitcast.84, s32[1280]{0:T(1024)S(1)} %eq.28, s32[80]{0:T(128)S(1)} %multiply_add_fusion), kind=kOutput, calls=%fused_computation.11 | convolution fusion | flops 264089600 | bytes 415040 | tf_op jit(solution)/shard_map/dot_general | solution.py:124
  (9 shorter events, 0.1 us)
Async XLA Ops:
  0.6 34.7 %copy-start = (bf16[10,80,1281]{2,1,0:T(8,128)(2,1)S(1)}, bf16[10,80,1281]{2,1,0:T(8,128)(2,1)}, u32[]{:S(2)}) copy-start(bf16[10,80,1281]{2,1,0:T(8,128)(2,1)} %param.6) | copy-start | bytes 6148804
  3.6 31.6 %all-to-all-start = ((bf16[64,10,2,80]{3,2,1,0:T(2,128)(2,1)}), bf16[64,10,2,80]{3,2,1,0:T(2,128)(2,1)S(1)}, u32[]{:S(2)}, u32[]{:S(2)}) async-start(bf16[64,10,2,80]{3,2,1,0:T(2,128)(2,1)} %bitcast.82), calls=%async_computation | async-start | bytes 655360 | tf_op jit(solution)/shard_map/all_to_all | solution.py:82
  36.2 15.7 %collective-permute-start.1 = (bf16[4,10,2,1281]{3,0,2,1:T(4,128)(2,1)S(1)}, bf16[4,10,2,1281]{3,0,2,1:T(4,128)(2,1)S(1)}, u32[]{:S(2)}, u32[]{:S(2)}) collective-permute-start(bf16[4,10,2,1281]{3,0,2,1:T(4,128)(2,1)S(1)} %get-tuple-element.11), channel_id=1, source_target_pairs={{64,0},{128,64},{192,128},{256,192},{320,256},{384,320},{448,384},... | collective-permute-start | bytes 614888 | tf_op jit(solution)/shard_map/ppermute | solution.py:95
  47.5 9.5 %collective-permute-start = (bf16[4,10,2,1281]{3,0,2,1:T(4,128)(2,1)S(1)}, bf16[4,10,2,1281]{3,0,2,1:T(4,128)(2,1)S(1)}, u32[]{:S(2)}, u32[]{:S(2)}) collective-permute-start(bf16[4,10,2,1281]{3,0,2,1:T(4,128)(2,1)S(1)} %get-tuple-element.10), channel_id=1, source_target_pairs={{0,64},{64,128},{128,192},{192,256},{256,320},{320,384},{384,448},... | collective-permute-start | bytes 614888 | tf_op jit(solution)/shard_map/ppermute | solution.py:94
  50.0 11.8 %copy-start.1 = (s32[640]{0:T(1024)S(1)}, s32[640]{0:T(1024)}, u32[]{:S(2)}) copy-start(s32[640]{0:T(1024)} %param.9) | copy-start | bytes 7684
  50.0 11.8 %copy-start.2 = (f32[2,8]{1,0:T(2,128)S(1)}, f32[2,8]{1,0:T(2,128)}, u32[]{:S(2)}) copy-start(f32[2,8]{1,0:T(2,128)} %param.8) | copy-start | bytes 196
  58.4 30.1 %all-to-all-start.1 = ((bf16[8,10,2,1281]{3,2,1,0:T(2,128)(2,1)}), bf16[8,10,2,1281]{3,2,1,0:T(2,128)(2,1)S(1)}, u32[]{:S(2)}, u32[]{:S(2)}) async-start(bf16[8,10,2,1281]{3,2,1,0:T(2,128)(2,1)} %copy.25), calls=%async_computation.1 | async-start | bytes 901120 | tf_op jit(solution)/shard_map/all_to_all | solution.py:102
  118.2 26.5 %all-to-all-start.2 = ((bf16[64,10,2,80]{3,2,1,0:T(2,128)(2,1)}), bf16[64,10,2,80]{3,2,1,0:T(2,128)(2,1)S(1)}, u32[]{:S(2)}, u32[]{:S(2)}) async-start(bf16[64,10,2,80]{3,2,1,0:T(2,128)(2,1)} %copy.28), calls=%async_computation.2 | async-start | bytes 655360 | tf_op jit(solution)/shard_map/all_to_all | solution.py:121

commit v6 on v5

--- a/solution.py
+++ b/solution.py
@@ -52,9 +52,14 @@
     lane = lax.broadcasted_iota(jnp.int32, (M, M), 1)
     return jnp.where(lane == order, 1.0, 0.0).astype(jnp.bfloat16)
 
-def gather_kernel(lat_ref, fourier_ref, quad_ref, owner_ref, out_ref):
+def gather_kernel(lat_ref, fourier_ref, quad_ref, owner_ref, out_ref, held_ref, arrival):
+    fetch = pltpu.make_async_copy(fourier_ref, held_ref, arrival)
+    fetch.start()
     order = row_orders(owner_ref)
-    moved = lax.dot_general(one_hot(order), fourier_ref[...], (((1,), (1,)), ((), ())), preferred_element_type=jnp.float32)
+    fetch.wait()
+    moved = lax.dot_general(
+        one_hot(order), held_ref[...], (((1,), (1,)), ((), ())), preferred_element_type=jnp.float32
+    )
     loop = lat_ref[0] * LOOPS + lax.broadcasted_iota(jnp.int32, (M, LOOPS), 1)
     out_ref[...] = jnp.where(order <= 2 * loop + 9, moved * quad_ref[...], 0.0).astype(jnp.bfloat16)
 
@@ -63,8 +68,9 @@
     return pl.pallas_call(
         gather_kernel,
         out_shape=jax.ShapeDtypeStruct((M, LOOPS), jnp.bfloat16),
-        in_specs=[pl.BlockSpec(memory_space=pltpu.SMEM), vm, vm, vm],
+        in_specs=[pl.BlockSpec(memory_space=pltpu.SMEM), pl.BlockSpec(memory_space=pl.ANY), vm, vm],
         out_specs=vm,
+        scratch_shapes=[pltpu.VMEM((LOOPS, M), jnp.bfloat16), pltpu.SemaphoreType.DMA],
         name="gather_rows",
     )(lat, fourier, quad, owner)
 

time: 147 us -> 148 us (level)
  no operation moved by 1% of the time
where the time goes in v6:
time: 148 us; the launch traced here: 147 us
  waiting for transfers between devices  53.5 us (36%)
  starting transfers between devices  48 us (32%)
  blocking collectives  25.6 us (17%)
  other arithmetic  5.19 us (4%)
  matrix products  4.59 us (3%)
  local copies, waits for them, and re-layouts  4.05 us (3%)
  Pallas kernels  3.53 us (2%)
  between operations  2.89 us (2%)
    all_gather x1, blocking collectives, body(): gathered = lax.all_gather(half, 'lat', axis=0, tiled=True)  25.6 us
    all_to_all x1, waiting for transfers between devices, body(): lax.all_to_all(merged, 'lat', split_axis=0, concat_axis=0, tiled=True, ax...  23.5 us
    all_to_all x1, starting transfers between devices, body(): lax.all_to_all(ordered, 'wave', split_axis=0, concat_axis=0, tiled=True)  18.2 us
    all_to_all x1, starting transfers between devices, body(): lax.all_to_all(synthesis, 'wave', split_axis=0, concat_axis=0, tiled=True)  13.2 us
    all_to_all x1, waiting for transfers between devices, body(): lax.all_to_all(ordered, 'wave', split_axis=0, concat_axis=0, tiled=True)  11.6 us
    all_to_all x1, waiting for transfers between devices, body(): lax.all_to_all(synthesis, 'wave', split_axis=0, concat_axis=0, tiled=True)  11.5 us
    ppermute x1, starting transfers between devices, body(): lax.ppermute(passed[SPLIT:], 'lat', [((i + 1) % n_lat, i) for i in range(...  11.3 us
    ppermute x1, waiting for transfers between devices, body(): lax.ppermute(passed[:SPLIT], 'lat', [(i, (i + 1) % n_lat) for i in range(...  5.05 us
  transfers between devices with their start and end apart: 5, of which 5 were waited for; matrix products, arithmetic and copies ran while one was open for 3% of the time, Pallas kernels for 0%

profile of v6, /device:TPU:1, one launch (start us, length us, event | category | flops | bytes accessed | tf_op | source)
XLA Modules:
  0.0 147.4 jit_solution(14983104124943974934)
XLA Ops:
  0.6 0.0 copy-start
  0.7 3.5 %gather_rows.1 = bf16[1280,80]{1,0:T(8,128)(2,1)} custom-call(s32[1]{0:T(128)} %bitcast.4.lat_ref, bf16[80,1280]{1,0:T(8,128)(2,1)} %bitcast.85, f32[1,80]{1,0:T(1,128)} %bitcast.87, s32[5,128]{1,0:T(8,128)} %bitcast.86), custom_call_target="tpu_custom_call" | custom-call | tf_op jit(solution)/shard_map/gather_rows/pallas_call | solution.py:68
  4.2 18.2 %all-to-all-start = ((bf16[64,10,2,80]{3,2,1,0:T(2,128)(2,1)}), bf16[64,10,2,80]{3,2,1,0:T(2,128)(2,1)S(1)}, u32[]{:S(2)}, u32[]{:S(2)}) async-start(bf16[64,10,2,80]{3,2,1,0:T(2,128)(2,1)} %bitcast.82), calls=%async_computation | async-start | bytes 655360 | tf_op jit(solution)/shard_map/all_to_all | solution.py:88
  22.4 0.8 broadcast_subtract_fusion.1
  23.2 0.2 iota_compare_fusion.9
  23.4 0.1 add_convert_fusion
  23.5 0.4 fusion.27
  23.9 0.1 stack.23
  24.0 0.1 bitcast_convert_fusion
  24.1 11.6 %all-to-all-done = bf16[64,10,2,80]{3,2,1,0:T(2,128)(2,1)S(1)} async-done(((bf16[64,10,2,80]{3,2,1,0:T(2,128)(2,1)}), bf16[64,10,2,80]{3,2,1,0:T(2,128)(2,1)S(1)}, u32[]{:S(2)}, u32[]{:S(2)}) %all-to-all-start) | async-done | bytes 204832 | tf_op jit(solution)/shard_map/all_to_all | solution.py:88
  35.7 0.2 constant_dynamic-slice_fusion.1
  36.0 0.0 copy-done
  36.0 0.6 fusion.1
  36.6 0.1 fusion.34
  36.8 11.3 %collective-permute-start.1 = (bf16[4,10,2,1281]{3,0,2,1:T(4,128)(2,1)S(1)}, bf16[4,10,2,1281]{3,0,2,1:T(4,128)(2,1)S(1)}, u32[]{:S(2)}, u32[]{:S(2)}) collective-permute-start(bf16[4,10,2,1281]{3,0,2,1:T(4,128)(2,1)S(1)} %get-tuple-element.11), channel_id=1, source_target_pairs={{64,0},{128,64},{192,128},{256,192},{320,256},{384,320},{448,384},... | collective-permute-start | bytes 614888 | tf_op jit(solution)/shard_map/ppermute | solution.py:101
  48.1 1.9 %collective-permute-start = (bf16[4,10,2,1281]{3,0,2,1:T(4,128)(2,1)S(1)}, bf16[4,10,2,1281]{3,0,2,1:T(4,128)(2,1)S(1)}, u32[]{:S(2)}, u32[]{:S(2)}) collective-permute-start(bf16[4,10,2,1281]{3,0,2,1:T(4,128)(2,1)S(1)} %get-tuple-element.10), channel_id=1, source_target_pairs={{0,64},{64,128},{128,192},{192,256},{256,320},{320,384},{384,448},... | collective-permute-start | bytes 614888 | tf_op jit(solution)/shard_map/ppermute | solution.py:100
  50.0 0.6 fusion.2
  50.6 0.0 copy-start.1
  50.6 0.0 copy-start.2
  50.7 1.9 %collective-permute-done.1 = bf16[4,10,2,1281]{3,0,2,1:T(4,128)(2,1)S(1)} collective-permute-done((bf16[4,10,2,1281]{3,0,2,1:T(4,128)(2,1)S(1)}, bf16[4,10,2,1281]{3,0,2,1:T(4,128)(2,1)S(1)}, u32[]{:S(2)}, u32[]{:S(2)}) %collective-permute-start.1) | collective-permute-done | bytes 204992 | tf_op jit(solution)/shard_map/ppermute | solution.py:101
  52.5 5.0 %collective-permute-done = bf16[4,10,2,1281]{3,0,2,1:T(4,128)(2,1)S(1)} collective-permute-done((bf16[4,10,2,1281]{3,0,2,1:T(4,128)(2,1)S(1)}, bf16[4,10,2,1281]{3,0,2,1:T(4,128)(2,1)S(1)}, u32[]{:S(2)}, u32[]{:S(2)}) %collective-permute-start) | collective-permute-done | bytes 204992 | tf_op jit(solution)/shard_map/ppermute | solution.py:100
  57.6 0.3 fusion.24
  57.8 1.1 copy.25
  59.0 3.5 %all-to-all-start.1 = ((bf16[8,10,2,1281]{3,2,1,0:T(2,128)(2,1)}), bf16[8,10,2,1281]{3,2,1,0:T(2,128)(2,1)S(1)}, u32[]{:S(2)}, u32[]{:S(2)}) async-start(bf16[8,10,2,1281]{3,2,1,0:T(2,128)(2,1)} %copy.25), calls=%async_computation.1 | async-start | bytes 901120 | tf_op jit(solution)/shard_map/all_to_all | solution.py:108
  62.4 0.0 copy-done.1
  62.5 0.0 copy-done.2
  62.5 0.6 constant_dynamic-slice_fusion
  65.1 0.2 copy.29
  65.2 0.2 eq.28
  65.5 23.5 %all-to-all-done.1 = bf16[8,10,2,1281]{3,2,1,0:T(2,128)(2,1)S(1)} async-done(((bf16[8,10,2,1281]{3,2,1,0:T(2,128)(2,1)}), bf16[8,10,2,1281]{3,2,1,0:T(2,128)(2,1)S(1)}, u32[]{:S(2)}, u32[]{:S(2)}) %all-to-all-start.1) | async-done | bytes 409952 | tf_op jit(solution)/shard_map/all_to_all | solution.py:108
  89.0 0.4 convert_reduce_fusion
  89.4 1.0 multiply_subtract_fusion
  90.4 0.1 select_convert_fusion
  90.5 25.6 %all_gather.3 = bf16[16,10,2,1281]{3,2,1,0:T(2,128)(2,1)S(1)} all-gather(bf16[1,10,2,1281]{3,2,1,0:T(2,128)(2,1)S(1)} %select_convert_fusion), channel_id=1, replica_groups=mesh['lat'=16,'wave'=64] {'lat'}, dimensions={0}, use_global_device_ids=true | all-gather | bytes 871080 | tf_op jit(solution)/shard_map/all_gather | solution.py:120
  116.2 0.1 copy.26
  116.3 1.1 fusion.19
  117.4 0.3 copy.27
  117.7 1.1 copy.28
  118.8 13.2 %all-to-all-start.2 = ((bf16[64,10,2,80]{3,2,1,0:T(2,128)(2,1)}), bf16[64,10,2,80]{3,2,1,0:T(2,128)(2,1)S(1)}, u32[]{:S(2)}, u32[]{:S(2)}) async-start(bf16[64,10,2,80]{3,2,1,0:T(2,128)(2,1)} %copy.28), calls=%async_computation.2 | async-start | bytes 655360 | tf_op jit(solution)/shard_map/all_to_all | solution.py:127
  132.0 1.0 bitcast_subtract_fusion
  133.0 0.8 maximum_bitcast_fusion
  133.8 11.5 %all-to-all-done.2 = bf16[64,10,2,80]{3,2,1,0:T(2,128)(2,1)S(1)} async-done(((bf16[64,10,2,80]{3,2,1,0:T(2,128)(2,1)}), bf16[64,10,2,80]{3,2,1,0:T(2,128)(2,1)S(1)}, u32[]{:S(2)}, u32[]{:S(2)}) %all-to-all-start.2) | async-done | bytes 204832 | tf_op jit(solution)/shard_map/all_to_all | solution.py:127
  145.3 2.2 %fusion.8 = bf16[1,80,1280]{2,1,0:T(8,128)(2,1)} fusion(bf16[1280,80]{1,0:T(8,128)(2,1)S(1)} %bitcast.84, s32[1280]{0:T(1024)S(1)} %eq.28, s32[80]{0:T(128)S(1)} %multiply_add_fusion), kind=kOutput, calls=%fused_computation.11 | convolution fusion | flops 264089600 | bytes 415040 | tf_op jit(solution)/shard_map/dot_general | solution.py:130
  (9 shorter events, 0.1 us)
Async XLA Ops:
  0.6 35.4 %copy-start = (bf16[10,80,1281]{2,1,0:T(8,128)(2,1)S(1)}, bf16[10,80,1281]{2,1,0:T(8,128)(2,1)}, u32[]{:S(2)}) copy-start(bf16[10,80,1281]{2,1,0:T(8,128)(2,1)} %param.6) | copy-start | bytes 6148804
  4.2 31.6 %all-to-all-start = ((bf16[64,10,2,80]{3,2,1,0:T(2,128)(2,1)}), bf16[64,10,2,80]{3,2,1,0:T(2,128)(2,1)S(1)}, u32[]{:S(2)}, u32[]{:S(2)}) async-start(bf16[64,10,2,80]{3,2,1,0:T(2,128)(2,1)} %bitcast.82), calls=%async_computation | async-start | bytes 655360 | tf_op jit(solution)/shard_map/all_to_all | solution.py:88
  36.8 15.7 %collective-permute-start.1 = (bf16[4,10,2,1281]{3,0,2,1:T(4,128)(2,1)S(1)}, bf16[4,10,2,1281]{3,0,2,1:T(4,128)(2,1)S(1)}, u32[]{:S(2)}, u32[]{:S(2)}) collective-permute-start(bf16[4,10,2,1281]{3,0,2,1:T(4,128)(2,1)S(1)} %get-tuple-element.11), channel_id=1, source_target_pairs={{64,0},{128,64},{192,128},{256,192},{320,256},{384,320},{448,384},... | collective-permute-start | bytes 614888 | tf_op jit(solution)/shard_map/ppermute | solution.py:101
  48.1 9.5 %collective-permute-start = (bf16[4,10,2,1281]{3,0,2,1:T(4,128)(2,1)S(1)}, bf16[4,10,2,1281]{3,0,2,1:T(4,128)(2,1)S(1)}, u32[]{:S(2)}, u32[]{:S(2)}) collective-permute-start(bf16[4,10,2,1281]{3,0,2,1:T(4,128)(2,1)S(1)} %get-tuple-element.10), channel_id=1, source_target_pairs={{0,64},{64,128},{128,192},{192,256},{256,320},{320,384},{384,448},... | collective-permute-start | bytes 614888 | tf_op jit(solution)/shard_map/ppermute | solution.py:100
  50.6 11.8 %copy-start.1 = (s32[640]{0:T(1024)S(1)}, s32[640]{0:T(1024)}, u32[]{:S(2)}) copy-start(s32[640]{0:T(1024)} %param.9) | copy-start | bytes 7684
  50.6 11.8 %copy-start.2 = (f32[2,8]{1,0:T(2,128)S(1)}, f32[2,8]{1,0:T(2,128)}, u32[]{:S(2)}) copy-start(f32[2,8]{1,0:T(2,128)} %param.8) | copy-start | bytes 196
  59.0 30.0 %all-to-all-start.1 = ((bf16[8,10,2,1281]{3,2,1,0:T(2,128)(2,1)}), bf16[8,10,2,1281]{3,2,1,0:T(2,128)(2,1)S(1)}, u32[]{:S(2)}, u32[]{:S(2)}) async-start(bf16[8,10,2,1281]{3,2,1,0:T(2,128)(2,1)} %copy.25), calls=%async_computation.1 | async-start | bytes 901120 | tf_op jit(solution)/shard_map/all_to_all | solution.py:108
  118.8 26.5 %all-to-all-start.2 = ((bf16[64,10,2,80]{3,2,1,0:T(2,128)(2,1)}), bf16[64,10,2,80]{3,2,1,0:T(2,128)(2,1)S(1)}, u32[]{:S(2)}, u32[]{:S(2)}) async-start(bf16[64,10,2,80]{3,2,1,0:T(2,128)(2,1)} %copy.28), calls=%async_computation.2 | async-start | bytes 655360 | tf_op jit(solution)/shard_map/all_to_all | solution.py:127
